TPU v7x, 512 devices: a whole 4x4x16 slice. The times are simulated.
512 devices in a mesh: tm: 16 (over z), height: 8 (over x, y_lo), width: 4 (over y_hi, core).
Axes of the slice: x: 4, y: 4 (y_hi: 2, y_lo: 2; y = y_hi * 2 + y_lo), z: 16, core: 2. Of those that a mesh axis runs over, the one named last changes fastest.
Arguments:
- video_in: bfloat16 [64, 64, 6144], P('tm', 'height', 'width'), may hold values from -24 to 24
- gain_first: float32 [96], replicated, may hold values from 0.5 to 2
- gain_second: float32 [192], replicated, may hold values from 0.5 to 2
- conv_first: bfloat16 [3, 3, 3, 96, 192], replicated, may hold values from -0.125 to 0.125
- conv_second: bfloat16 [3, 3, 3, 192, 192], replicated, may hold values from -0.078125 to 0.078125
- shortcut: bfloat16 [96, 192], replicated, may hold values from -0.625 to 0.625
- downscale_weight: bfloat16 [3, 3, 192, 192], replicated, may hold values from -0.15625 to 0.15625
Outputs:
- encoded: bfloat16 [64, 32, 6144], P('tm', 'height', 'width')
All inputs are finite; a program needn't handle non-finite values.
Results may differ from a plain program's by a relative error of at most 0.0054.
Values may be sent and summed in bfloat16 or wider, within the bound.
A program may use at most 64 MiB of HBM per device.

v0:
```python
import jax
import jax.numpy as jnp
from jax import lax
from jax.sharding import PartitionSpec as P

epsilon = 1e-06


def shifted(value, axis, by):
    devices = lax.axis_size(axis)
    pairs = [(i, i + by) for i in range(devices) if 0 <= i + by < devices]
    return lax.ppermute(value, axis, pairs)


def padded(block, sides, width):
    for axis, dim in sides:
        count = lax.axis_size(axis)
        forward = [(i, i + 1) for i in range(count - 1)]
        backward = [(target, source) for source, target in forward]
        low = lax.ppermute(
            lax.slice_in_dim(block, block.shape[dim] - width, None, axis=dim), axis, forward
        )
        high = lax.ppermute(lax.slice_in_dim(block, 0, width, axis=dim), axis, backward)
        block = jnp.concatenate([low, block, high], axis=dim)
    return block


def activate(feature_values, gain):
    feature_values = feature_values.astype(jnp.float32)
    meansq = jnp.mean(feature_values * feature_values, axis=-1, keepdims=True)
    normed = feature_values * lax.rsqrt(meansq + epsilon) * gain
    return jax.nn.silu(normed).astype(jnp.bfloat16)


def convolve(border_filled, filter_weight):
    frames = border_filled.shape[0] - 2
    rows = border_filled.shape[1] - 2
    cols = border_filled.shape[2] - 2
    c_in = border_filled.shape[3]
    c_out = filter_weight.shape[4]
    total = jnp.zeros((frames * rows * cols, c_out), jnp.float32)
    for depth_tap in range(3):
        for row_tap in range(3):
            window_slab = border_filled[depth_tap : depth_tap + frames, row_tap : row_tap + rows]
            stacked = jnp.concatenate(
                [window_slab[:, :, col_tap : col_tap + cols] for col_tap in range(3)], axis=-1
            )
            total = total + jnp.dot(
                stacked.reshape(-1, 3 * c_in),
                filter_weight[depth_tap, row_tap].reshape(3 * c_in, c_out),
                preferred_element_type=jnp.float32,
            )
    return total.reshape(frames, rows, cols, c_out)


def halve_spatial(border_filled, filter_weight):
    frames = border_filled.shape[0]
    out_rows = (border_filled.shape[1] - 1) // 2
    out_cols = (border_filled.shape[2] - 1) // 2
    chans = border_filled.shape[3]
    total = jnp.zeros((frames * out_rows * out_cols, filter_weight.shape[3]), jnp.float32)
    for row_tap in range(3):
        stacked = jnp.concatenate(
            [
                border_filled[
                    :, row_tap : row_tap + 2 * out_rows : 2, col_tap : col_tap + 2 * out_cols : 2
                ]
                for col_tap in range(3)
            ],
            axis=-1,
        )
        total = total + jnp.dot(
            stacked.reshape(-1, 3 * chans),
            filter_weight[row_tap].reshape(3 * chans, filter_weight.shape[3]),
            preferred_element_type=jnp.float32,
        )
    return total.reshape(frames, out_rows, out_cols, filter_weight.shape[3])


def local(video_in, gain_first, gain_second, conv_first, conv_second, shortcut, downscale_weight):
    frames, rows, merged_cols = video_in.shape
    c_in = gain_first.shape[0]
    c_out = gain_second.shape[0]
    cols = merged_cols // c_in
    field = video_in.reshape(frames, rows, cols, c_in)
    first = activate(field, gain_first)
    earlier = shifted(first[frames - 2 :], "tm", 1)
    framed = jnp.concatenate([earlier, first], axis=0)
    border_filled = padded(framed, (("height", 1), ("width", 2)), 1)
    hidden = convolve(border_filled, conv_first)
    second = activate(hidden, gain_second)
    earlier_mid = shifted(second[frames - 2 :], "tm", 1)
    framed_mid = jnp.concatenate([earlier_mid, second], axis=0)
    padded_mid = padded(framed_mid, (("height", 1), ("width", 2)), 1)
    branch = convolve(padded_mid, conv_second)
    skip_term = jnp.dot(
        field.reshape(-1, c_in), shortcut, preferred_element_type=jnp.float32
    ).reshape(frames, rows, cols, c_out)
    merged = (branch + skip_term).astype(jnp.bfloat16)
    next_col = shifted(merged[:, :, :1], "width", -1)
    widened = jnp.concatenate([merged, next_col], axis=2)
    next_row = shifted(widened[:, :1], "height", -1)
    border_filled_output = jnp.concatenate([widened, next_row], axis=1)
    block_output = halve_spatial(border_filled_output, downscale_weight)
    return block_output.astype(jnp.bfloat16).reshape(frames, rows // 2, cols // 2 * c_out)


def solution(mesh):
    placed = (P("tm", "height", "width"), P(), P(), P(), P(), P(), P())
    return jax.shard_map(
        local, mesh=mesh, in_specs=placed, out_specs=P("tm", "height", "width"), check_vma=False
    )
```

profile of v0, /device:TPU:257, one launch (start us, length us, event | category | flops | bytes accessed | tf_op | source)
XLA Modules:
  0.0 91.2 jit_solution(16514862410478673716)
XLA Ops:
  0.0 1.1 %reshape.106 = bf16[4,8,16,96]{3,2,1,0:T(8,128)(2,1)S(1)} reshape(bf16[4,8,1536]{2,1,0:T(8,128)(2,1)} %param.7) | data formatting | bytes 196608 | tf_op jit(solution)/shard_map/reshape | solution.py:85
  2.1 2.6 %collective-permute-start = (bf16[2,8,16,96]{3,2,1,0:T(8,128)(2,1)S(1)}, bf16[2,8,16,96]{3,2,1,0:T(8,128)(2,1)S(1)}, u32[]{:S(2)}, u32[]{:S(2)}) collective-permute-start(bf16[2,8,16,96]{3,2,1,0:T(8,128)(2,1)S(1)} %slice.522), channel_id=1, source_target_pairs={{0,32},{32,64},{64,96},{96,128},{128,160},{160,192},{192,224},{224... | collective-permute-start | bytes 147464 | tf_op jit(solution)/shard_map/ppermute | solution.py:12
  4.7 1.5 %fusion.19 = (bf16[1,1,3,96,192]{4,3,2,1,0:T(8,128)(2,1)S(1)}, bf16[1,1,3,96,192]{4,3,2,1,0:T(8,128)(2,1)S(1)}, bf16[1,1,3,96,192]{4,3,2,1,0:T(8,128)(2,1)S(1)},...) fusion(bf16[3,3,3,96,192]{4,3,2,1,0:T(8,128)(2,1)} %param.10), kind=kLoop, calls=%fused_computation.93 | loop fusion | bytes 1990656 | tf_op jit(solution)/shard_map/slice | solution.py:50
  6.2 2.1 %collective-permute-done = bf16[2,8,16,96]{3,2,1,0:T(8,128)(2,1)S(1)} collective-permute-done((bf16[2,8,16,96]{3,2,1,0:T(8,128)(2,1)S(1)}, bf16[2,8,16,96]{3,2,1,0:T(8,128)(2,1)S(1)}, u32[]{:S(2)}, u32[]{:S(2)}) %collective-permute-start) | collective-permute-done | bytes 49184 | tf_op jit(solution)/shard_map/ppermute | solution.py:12
  8.3 3.2 %collective-permute-start.1 = (bf16[6,1,16,96]{3,2,1,0:T(8,128)(2,1)S(1)}, bf16[6,1,16,96]{3,2,1,0:T(8,128)(2,1)S(1)}, u32[]{:S(2)}, u32[]{:S(2)}) collective-permute-start(bf16[6,1,16,96]{3,2,1,0:T(8,128)(2,1)S(1)} %get-tuple-element.90), channel_id=1, source_target_pairs={{0,4},{4,8},{8,12},{12,16},{16,20},{20,24},{24,28},{1,5},{5,9},{9,... | collective-permute-start | bytes 55304 | tf_op jit(solution)/shard_map/ppermute | solution.py:20
  11.5 1.3 %collective-permute-start.2 = (bf16[6,1,16,96]{3,2,1,0:T(8,128)(2,1)S(1)}, bf16[6,1,16,96]{3,2,1,0:T(8,128)(2,1)S(1)}, u32[]{:S(2)}, u32[]{:S(2)}) collective-permute-start(bf16[6,1,16,96]{3,2,1,0:T(8,128)(2,1)S(1)} %get-tuple-element.91), channel_id=1, source_target_pairs={{4,0},{8,4},{12,8},{16,12},{20,16},{24,20},{28,24},{5,1},{9,5},{13... | collective-permute-start | bytes 55304 | tf_op jit(solution)/shard_map/ppermute | solution.py:23
  12.9 3.2 %collective-permute-done.2 = bf16[6,1,16,96]{3,2,1,0:T(8,128)(2,1)S(1)} collective-permute-done((bf16[6,1,16,96]{3,2,1,0:T(8,128)(2,1)S(1)}, bf16[6,1,16,96]{3,2,1,0:T(8,128)(2,1)S(1)}, u32[]{:S(2)}, u32[]{:S(2)}) %collective-permute-start.2) | collective-permute-done | bytes 18464 | tf_op jit(solution)/shard_map/ppermute | solution.py:23
  16.2 7.7 %collective-permute-start.3 = (bf16[6,10,1,96]{3,2,1,0:T(2,128)(2,1)S(1)}, bf16[6,10,1,96]{3,2,1,0:T(2,128)(2,1)S(1)}, u32[]{:S(2)}, u32[]{:S(2)}) collective-permute-start(bf16[6,10,1,96]{3,2,1,0:T(2,128)(2,1)S(1)} %get-tuple-element.80), channel_id=1, source_target_pairs={{0,1},{1,2},{2,3},{4,5},{5,6},{6,7},{8,9},{9,10},{10,11},{12,13},{... | collective-permute-start | bytes 34568 | tf_op jit(solution)/shard_map/ppermute | solution.py:20
  23.8 1.9 %collective-permute-start.4 = (bf16[6,10,1,96]{3,2,1,0:T(2,128)(2,1)S(1)}, bf16[6,10,1,96]{3,2,1,0:T(2,128)(2,1)S(1)}, u32[]{:S(2)}, u32[]{:S(2)}) collective-permute-start(bf16[6,10,1,96]{3,2,1,0:T(2,128)(2,1)S(1)} %get-tuple-element.81), channel_id=1, source_target_pairs={{1,0},{2,1},{3,2},{5,4},{6,5},{7,6},{9,8},{10,9},{11,10},{13,12},{... | collective-permute-start | bytes 34568 | tf_op jit(solution)/shard_map/ppermute | solution.py:23
  26.0 4.6 %collective-permute-done.4 = bf16[6,10,1,96]{3,2,1,0:T(2,128)(2,1)S(1)} collective-permute-done((bf16[6,10,1,96]{3,2,1,0:T(2,128)(2,1)S(1)}, bf16[6,10,1,96]{3,2,1,0:T(2,128)(2,1)S(1)}, u32[]{:S(2)}, u32[]{:S(2)}) %collective-permute-start.4) | collective-permute-done | bytes 11552 | tf_op jit(solution)/shard_map/ppermute | solution.py:23
  35.7 1.1 %multiply_reduce_fusion = (f32[512]{0:T(512)S(1)}, f32[512,192]{0,1:T(8,128)}) fusion(f32[512,192]{0,1:T(8,128)S(1)} %convolution_add_fusion.2, bf16[512,288]{1,0:T(8,128)(2,1)S(1)} %bitcast.104, bf16[288,192]{1,0:T(8,128)(2,1)S(1)} %bitcast.128), kind=kOutput, calls=%fused_computation.54 | convolution fusion | flops 56917504 | bytes 1193984 | tf_op jit(solution)/shard_map/dot_general | solution.py:48
  36.8 1.2 %copy.9 = f32[512,192]{1,0:T(8,128)S(1)} copy(f32[512,192]{0,1:T(8,128)} %get-tuple-element.95) | data formatting | bytes 786432 | tf_op jit(solution)/shard_map/add | solution.py:48
  38.3 1.9 %collective-permute-start.5 = (bf16[2,8,16,192]{3,2,1,0:T(8,128)(2,1)S(1)}, bf16[2,8,16,192]{3,2,1,0:T(8,128)(2,1)S(1)}, u32[]{:S(2)}, u32[]{:S(2)}) collective-permute-start(bf16[2,8,16,192]{3,2,1,0:T(8,128)(2,1)S(1)} %slice.549), channel_id=1, source_target_pairs={{0,32},{32,64},{64,96},{96,128},{128,160},{160,192},{192,224},{224... | collective-permute-start | bytes 294920 | tf_op jit(solution)/shard_map/ppermute | solution.py:12
  40.5 4.8 %collective-permute-done.5 = bf16[2,8,16,192]{3,2,1,0:T(8,128)(2,1)S(1)} collective-permute-done((bf16[2,8,16,192]{3,2,1,0:T(8,128)(2,1)S(1)}, bf16[2,8,16,192]{3,2,1,0:T(8,128)(2,1)S(1)}, u32[]{:S(2)}, u32[]{:S(2)}) %collective-permute-start.5) | collective-permute-done | bytes 98336 | tf_op jit(solution)/shard_map/ppermute | solution.py:12
  45.3 3.6 %collective-permute-start.6 = (bf16[6,1,16,192]{3,2,1,0:T(8,128)(2,1)S(1)}, bf16[6,1,16,192]{3,2,1,0:T(8,128)(2,1)S(1)}, u32[]{:S(2)}, u32[]{:S(2)}) collective-permute-start(bf16[6,1,16,192]{3,2,1,0:T(8,128)(2,1)S(1)} %get-tuple-element.56), channel_id=1, source_target_pairs={{0,4},{4,8},{8,12},{12,16},{16,20},{20,24},{24,28},{1,5},{5,9},{9,... | collective-permute-start | bytes 110600 | tf_op jit(solution)/shard_map/ppermute | solution.py:20
  48.9 1.3 %collective-permute-start.7 = (bf16[6,1,16,192]{3,2,1,0:T(8,128)(2,1)S(1)}, bf16[6,1,16,192]{3,2,1,0:T(8,128)(2,1)S(1)}, u32[]{:S(2)}, u32[]{:S(2)}) collective-permute-start(bf16[6,1,16,192]{3,2,1,0:T(8,128)(2,1)S(1)} %get-tuple-element.57), channel_id=1, source_target_pairs={{4,0},{8,4},{12,8},{16,12},{20,16},{24,20},{28,24},{5,1},{9,5},{13... | collective-permute-start | bytes 110600 | tf_op jit(solution)/shard_map/ppermute | solution.py:23
  50.3 3.5 %collective-permute-done.7 = bf16[6,1,16,192]{3,2,1,0:T(8,128)(2,1)S(1)} collective-permute-done((bf16[6,1,16,192]{3,2,1,0:T(8,128)(2,1)S(1)}, bf16[6,1,16,192]{3,2,1,0:T(8,128)(2,1)S(1)}, u32[]{:S(2)}, u32[]{:S(2)}) %collective-permute-start.7) | collective-permute-done | bytes 36896 | tf_op jit(solution)/shard_map/ppermute | solution.py:23
  54.1 5.1 %collective-permute-start.8 = (bf16[6,10,1,192]{3,2,1,0:T(2,128)(2,1)S(1)}, bf16[6,10,1,192]{3,2,1,0:T(2,128)(2,1)S(1)}, u32[]{:S(2)}, u32[]{:S(2)}) collective-permute-start(bf16[6,10,1,192]{3,2,1,0:T(2,128)(2,1)S(1)} %get-tuple-element.46), channel_id=1, source_target_pairs={{0,1},{1,2},{2,3},{4,5},{5,6},{6,7},{8,9},{9,10},{10,11},{12,13},{... | collective-permute-start | bytes 69128 | tf_op jit(solution)/shard_map/ppermute | solution.py:20
  59.2 2.1 %collective-permute-start.9 = (bf16[6,10,1,192]{3,2,1,0:T(2,128)(2,1)S(1)}, bf16[6,10,1,192]{3,2,1,0:T(2,128)(2,1)S(1)}, u32[]{:S(2)}, u32[]{:S(2)}) collective-permute-start(bf16[6,10,1,192]{3,2,1,0:T(2,128)(2,1)S(1)} %get-tuple-element.47), channel_id=1, source_target_pairs={{1,0},{2,1},{3,2},{5,4},{6,5},{7,6},{9,8},{10,9},{11,10},{13,12},{... | collective-permute-start | bytes 69128 | tf_op jit(solution)/shard_map/ppermute | solution.py:23
  61.4 4.9 %collective-permute-done.9 = bf16[6,10,1,192]{3,2,1,0:T(2,128)(2,1)S(1)} collective-permute-done((bf16[6,10,1,192]{3,2,1,0:T(2,128)(2,1)S(1)}, bf16[6,10,1,192]{3,2,1,0:T(2,128)(2,1)S(1)}, u32[]{:S(2)}, u32[]{:S(2)}) %collective-permute-start.9) | collective-permute-done | bytes 23072 | tf_op jit(solution)/shard_map/ppermute | solution.py:23
  73.4 1.9 %collective-permute-start.10 = (bf16[4,8,1,192]{3,2,1,0:T(2,128)(2,1)S(1)}, bf16[4,8,1,192]{3,2,1,0:T(2,128)(2,1)S(1)}, u32[]{:S(2)}, u32[]{:S(2)}) collective-permute-start(bf16[4,8,1,192]{3,2,1,0:T(2,128)(2,1)S(1)} %slice.576), channel_id=1, source_target_pairs={{1,0},{2,1},{3,2},{5,4},{6,5},{7,6},{9,8},{10,9},{11,10},{13,12},{... | collective-permute-start | bytes 36872 | tf_op jit(solution)/shard_map/ppermute | solution.py:12
  75.8 4.3 %collective-permute-done.10 = bf16[4,8,1,192]{3,2,1,0:T(2,128)(2,1)S(1)} collective-permute-done((bf16[4,8,1,192]{3,2,1,0:T(2,128)(2,1)S(1)}, bf16[4,8,1,192]{3,2,1,0:T(2,128)(2,1)S(1)}, u32[]{:S(2)}, u32[]{:S(2)}) %collective-permute-start.10) | collective-permute-done | bytes 12320 | tf_op jit(solution)/shard_map/ppermute | solution.py:12
  81.2 1.3 %collective-permute-start.11 = (bf16[4,1,17,192]{3,2,1,0:T(8,128)(2,1)S(1)}, bf16[4,1,17,192]{3,2,1,0:T(8,128)(2,1)S(1)}, u32[]{:S(2)}, u32[]{:S(2)}) collective-permute-start(bf16[4,1,17,192]{3,2,1,0:T(8,128)(2,1)S(1)} %fusion.16), channel_id=1, source_target_pairs={{4,0},{8,4},{12,8},{16,12},{20,16},{24,20},{28,24},{5,1},{9,5},{13... | collective-permute-start | bytes 78344 | tf_op jit(solution)/shard_map/ppermute | solution.py:12
  82.9 3.1 %collective-permute-done.11 = bf16[4,1,17,192]{3,2,1,0:T(8,128)(2,1)S(1)} collective-permute-done((bf16[4,1,17,192]{3,2,1,0:T(8,128)(2,1)S(1)}, bf16[4,1,17,192]{3,2,1,0:T(8,128)(2,1)S(1)}, u32[]{:S(2)}, u32[]{:S(2)}) %collective-permute-start.11) | collective-permute-done | bytes 26144 | tf_op jit(solution)/shard_map/ppermute | solution.py:12
  (94 shorter events, 21.3 us)
Async XLA Ops:
  0.0 73.2 %copy-start = (bf16[96,192]{1,0:T(8,128)(2,1)S(1)}, bf16[96,192]{1,0:T(8,128)(2,1)}, u32[]{:S(2)}) copy-start(bf16[96,192]{1,0:T(8,128)(2,1)} %param.12) | copy-start | bytes 110596
  2.1 6.2 %collective-permute-start = (bf16[2,8,16,96]{3,2,1,0:T(8,128)(2,1)S(1)}, bf16[2,8,16,96]{3,2,1,0:T(8,128)(2,1)S(1)}, u32[]{:S(2)}, u32[]{:S(2)}) collective-permute-start(bf16[2,8,16,96]{3,2,1,0:T(8,128)(2,1)S(1)} %slice.522), channel_id=1, source_target_pairs={{0,32},{32,64},{64,96},{96,128},{128,160},{160,192},{192,224},{224... | collective-permute-start | bytes 147464 | tf_op jit(solution)/shard_map/ppermute | solution.py:12
  8.3 4.6 %collective-permute-start.1 = (bf16[6,1,16,96]{3,2,1,0:T(8,128)(2,1)S(1)}, bf16[6,1,16,96]{3,2,1,0:T(8,128)(2,1)S(1)}, u32[]{:S(2)}, u32[]{:S(2)}) collective-permute-start(bf16[6,1,16,96]{3,2,1,0:T(8,128)(2,1)S(1)} %get-tuple-element.90), channel_id=1, source_target_pairs={{0,4},{4,8},{8,12},{12,16},{16,20},{20,24},{24,28},{1,5},{5,9},{9,... | collective-permute-start | bytes 55304 | tf_op jit(solution)/shard_map/ppermute | solution.py:20
  11.5 4.6 %collective-permute-start.2 = (bf16[6,1,16,96]{3,2,1,0:T(8,128)(2,1)S(1)}, bf16[6,1,16,96]{3,2,1,0:T(8,128)(2,1)S(1)}, u32[]{:S(2)}, u32[]{:S(2)}) collective-permute-start(bf16[6,1,16,96]{3,2,1,0:T(8,128)(2,1)S(1)} %get-tuple-element.91), channel_id=1, source_target_pairs={{4,0},{8,4},{12,8},{16,12},{20,16},{24,20},{28,24},{5,1},{9,5},{13... | collective-permute-start | bytes 55304 | tf_op jit(solution)/shard_map/ppermute | solution.py:23
  16.2 9.8 %collective-permute-start.3 = (bf16[6,10,1,96]{3,2,1,0:T(2,128)(2,1)S(1)}, bf16[6,10,1,96]{3,2,1,0:T(2,128)(2,1)S(1)}, u32[]{:S(2)}, u32[]{:S(2)}) collective-permute-start(bf16[6,10,1,96]{3,2,1,0:T(2,128)(2,1)S(1)} %get-tuple-element.80), channel_id=1, source_target_pairs={{0,1},{1,2},{2,3},{4,5},{5,6},{6,7},{8,9},{9,10},{10,11},{12,13},{... | collective-permute-start | bytes 34568 | tf_op jit(solution)/shard_map/ppermute | solution.py:20
  23.8 6.7 %collective-permute-start.4 = (bf16[6,10,1,96]{3,2,1,0:T(2,128)(2,1)S(1)}, bf16[6,10,1,96]{3,2,1,0:T(2,128)(2,1)S(1)}, u32[]{:S(2)}, u32[]{:S(2)}) collective-permute-start(bf16[6,10,1,96]{3,2,1,0:T(2,128)(2,1)S(1)} %get-tuple-element.81), channel_id=1, source_target_pairs={{1,0},{2,1},{3,2},{5,4},{6,5},{7,6},{9,8},{10,9},{11,10},{13,12},{... | collective-permute-start | bytes 34568 | tf_op jit(solution)/shard_map/ppermute | solution.py:23
  35.7 2.4 %copy-start.3 = (f32[192]{0:T(256)S(1)}, f32[192]{0:T(256)}, u32[]{:S(2)}) copy-start(f32[192]{0:T(256)} %param.9) | copy-start | bytes 2308
  35.7 4.5 %copy-start.1 = (bf16[3,3,3,192,192]{4,3,2,1,0:T(8,128)(2,1)S(1)}, bf16[3,3,3,192,192]{4,3,2,1,0:T(8,128)(2,1)}, u32[]{:S(2)}) copy-start(bf16[3,3,3,192,192]{4,3,2,1,0:T(8,128)(2,1)} %param.11) | copy-start | bytes 5971972
  38.3 6.9 %collective-permute-start.5 = (bf16[2,8,16,192]{3,2,1,0:T(8,128)(2,1)S(1)}, bf16[2,8,16,192]{3,2,1,0:T(8,128)(2,1)S(1)}, u32[]{:S(2)}, u32[]{:S(2)}) collective-permute-start(bf16[2,8,16,192]{3,2,1,0:T(8,128)(2,1)S(1)} %slice.549), channel_id=1, source_target_pairs={{0,32},{32,64},{64,96},{96,128},{128,160},{160,192},{192,224},{224... | collective-permute-start | bytes 294920 | tf_op jit(solution)/shard_map/ppermute | solution.py:12
  45.3 5.0 %collective-permute-start.6 = (bf16[6,1,16,192]{3,2,1,0:T(8,128)(2,1)S(1)}, bf16[6,1,16,192]{3,2,1,0:T(8,128)(2,1)S(1)}, u32[]{:S(2)}, u32[]{:S(2)}) collective-permute-start(bf16[6,1,16,192]{3,2,1,0:T(8,128)(2,1)S(1)} %get-tuple-element.56), channel_id=1, source_target_pairs={{0,4},{4,8},{8,12},{12,16},{16,20},{20,24},{24,28},{1,5},{5,9},{9,... | collective-permute-start | bytes 110600 | tf_op jit(solution)/shard_map/ppermute | solution.py:20
  48.9 4.8 %collective-permute-start.7 = (bf16[6,1,16,192]{3,2,1,0:T(8,128)(2,1)S(1)}, bf16[6,1,16,192]{3,2,1,0:T(8,128)(2,1)S(1)}, u32[]{:S(2)}, u32[]{:S(2)}) collective-permute-start(bf16[6,1,16,192]{3,2,1,0:T(8,128)(2,1)S(1)} %get-tuple-element.57), channel_id=1, source_target_pairs={{4,0},{8,4},{12,8},{16,12},{20,16},{24,20},{28,24},{5,1},{9,5},{13... | collective-permute-start | bytes 110600 | tf_op jit(solution)/shard_map/ppermute | solution.py:23
  54.1 7.3 %collective-permute-start.8 = (bf16[6,10,1,192]{3,2,1,0:T(2,128)(2,1)S(1)}, bf16[6,10,1,192]{3,2,1,0:T(2,128)(2,1)S(1)}, u32[]{:S(2)}, u32[]{:S(2)}) collective-permute-start(bf16[6,10,1,192]{3,2,1,0:T(2,128)(2,1)S(1)} %get-tuple-element.46), channel_id=1, source_target_pairs={{0,1},{1,2},{2,3},{4,5},{5,6},{6,7},{8,9},{9,10},{10,11},{12,13},{... | collective-permute-start | bytes 69128 | tf_op jit(solution)/shard_map/ppermute | solution.py:20
  59.2 7.0 %collective-permute-start.9 = (bf16[6,10,1,192]{3,2,1,0:T(2,128)(2,1)S(1)}, bf16[6,10,1,192]{3,2,1,0:T(2,128)(2,1)S(1)}, u32[]{:S(2)}, u32[]{:S(2)}) collective-permute-start(bf16[6,10,1,192]{3,2,1,0:T(2,128)(2,1)S(1)} %get-tuple-element.47), channel_id=1, source_target_pairs={{1,0},{2,1},{3,2},{5,4},{6,5},{7,6},{9,8},{10,9},{11,10},{13,12},{... | collective-permute-start | bytes 69128 | tf_op jit(solution)/shard_map/ppermute | solution.py:23
  72.9 2.4 %copy-start.2 = (bf16[3,3,192,192]{3,2,1,0:T(8,128)(2,1)S(1)}, bf16[3,3,192,192]{3,2,1,0:T(8,128)(2,1)}, u32[]{:S(2)}) copy-start(bf16[3,3,192,192]{3,2,1,0:T(8,128)(2,1)} %param.13) | copy-start | bytes 1990660
  73.4 6.7 %collective-permute-start.10 = (bf16[4,8,1,192]{3,2,1,0:T(2,128)(2,1)S(1)}, bf16[4,8,1,192]{3,2,1,0:T(2,128)(2,1)S(1)}, u32[]{:S(2)}, u32[]{:S(2)}) collective-permute-start(bf16[4,8,1,192]{3,2,1,0:T(2,128)(2,1)S(1)} %slice.576), channel_id=1, source_target_pairs={{1,0},{2,1},{3,2},{5,4},{6,5},{7,6},{9,8},{10,9},{11,10},{13,12},{... | collective-permute-start | bytes 36872 | tf_op jit(solution)/shard_map/ppermute | solution.py:12
  81.2 4.8 %collective-permute-start.11 = (bf16[4,1,17,192]{3,2,1,0:T(8,128)(2,1)S(1)}, bf16[4,1,17,192]{3,2,1,0:T(8,128)(2,1)S(1)}, u32[]{:S(2)}, u32[]{:S(2)}) collective-permute-start(bf16[4,1,17,192]{3,2,1,0:T(8,128)(2,1)S(1)} %fusion.16), channel_id=1, source_target_pairs={{4,0},{8,4},{12,8},{16,12},{20,16},{24,20},{28,24},{5,1},{9,5},{13... | collective-permute-start | bytes 78344 | tf_op jit(solution)/shard_map/ppermute | solution.py:12
where the time goes:
time: 91.7 us; the launch traced here: 91.2 us
  starting transfers between devices  34 us (37%)
  waiting for transfers between devices  30.4 us (33%)
  local copies, waits for them, and re-layouts  11.1 us (12%)
  matrix products  8.17 us (9%)
  other arithmetic  6.84 us (7%)
    ppermute x4, starting transfers between devices, padded(): lax.ppermute(lax.slice_in_dim(block, block.shape[dim] - width, None, axis...  19.6 us
    ppermute x4, waiting for transfers between devices, padded(): lax.ppermute(lax.slice_in_dim(block, 0, width, axis=dim), axis, backward)  16.1 us
    ppermute x4, waiting for transfers between devices, shifted(): return lax.ppermute(value, axis, pairs)  14.3 us
    ppermute x4, starting transfers between devices, shifted(): return lax.ppermute(value, axis, pairs)  7.78 us
    dot_general x18, matrix products, convolve(): jnp.dot(stacked.reshape(-1, 3 * c_in), filter_weight[depth_tap, row_tap]....  7.06 us
    ppermute x4, starting transfers between devices, padded(): lax.ppermute(lax.slice_in_dim(block, 0, width, axis=dim), axis, backward)  6.61 us
    slice x9, local copies, waits for them, and re-layouts, halve_spatial(): border_filled[:, row_tap:row_tap + 2 * out_rows:2, col_tap:col_tap + 2 *...  4.66 us
    concatenate x16, other arithmetic, convolve(): jnp.concatenate([window_slab[:, :, col_tap:col_tap + cols] for col_tap in...  3.96 us
  transfers between devices with their start and end apart: 12, of which 8 were waited for; matrix products, arithmetic and copies ran while one was open for 3% of the time, Pallas kernels for 0%

commit v1 on v0

v1 whole, which is shorter than its diff:
```python
import functools

import jax
import jax.numpy as jnp
from jax import lax
from jax.experimental import pallas as pl
from jax.experimental.pallas import tpu as pltpu
from jax.sharding import PartitionSpec as P

MESH = pl.DeviceIdType.MESH
epsilon = 1e-06
SIDES = [(-1, 0), (1, 0), (0, -1), (0, 1), (-1, -1), (-1, 1), (1, -1), (1, 1)]


def halo_kernel(x_ref, zb_ref, rb_ref, cl_ref, cr_ref, kl_ref, kr_ref, zs, zr, ss, sr):
    t, h, w = lax.axis_index("tm"), lax.axis_index("height"), lax.axis_index("width")
    nt, nh, nw = lax.axis_size("tm"), lax.axis_size("height"), lax.axis_size("width")

    def exists(dh, dw):
        ok = None
        for pos, by, n in ((h, dh, nh), (w, dw, nw)):
            if by:
                one = pos > 0 if by < 0 else pos < n - 1
                ok = one if ok is None else jnp.logical_and(ok, one)
        return ok

    def part(dh, dw):
        rows = {-1: pl.ds(0, 4), 0: pl.ds(0, 8), 1: pl.ds(6, 2)}[dh]
        lanes = {-1: pl.ds(0, 384), 0: pl.ds(0, 1536), 1: pl.ds(1152, 384)}[dw]
        return rows, lanes

    def landing(dh, dw):
        if dw == 0:
            return rb_ref, pl.ds(0, 1536)
        if dh == 0:
            return (cl_ref if dw == 1 else cr_ref), pl.ds(0, 384)
        return (kl_ref if dw == 1 else kr_ref), pl.ds(0, 384)

    bar = pltpu.get_barrier_semaphore()
    count = jnp.int32(0)
    for dh, dw in SIDES:
        ok = exists(dh, dw)
        count += ok.astype(jnp.int32)

        @pl.when(ok)
        def _():
            pl.semaphore_signal(bar, inc=1, device_id=(t, h + dh, w + dw), device_id_type=MESH)

    for dt in (-1, 1):
        ok = t > 0 if dt < 0 else t < nt - 1
        count += ok.astype(jnp.int32)

        @pl.when(ok)
        def _():
            pl.semaphore_signal(bar, inc=1, device_id=(t + dt, h, w), device_id_type=MESH)

    @pl.when(t == 0)
    def _():
        zb_ref[...] = jnp.zeros_like(zb_ref)
        for ref in (rb_ref, cl_ref, cr_ref, kl_ref, kr_ref):
            ref[pl.ds(0, 4)] = jnp.zeros((4,) + ref.shape[1:], ref.dtype)

    def clear(ref, rows, n):
        ref[:, pl.ds(rows, n), :] = jnp.zeros((8, n, ref.shape[2]), ref.dtype)

    @pl.when(h == 0)
    def _():
        for ref in (rb_ref, kl_ref, kr_ref):
            clear(ref, 6, 2)

    @pl.when(h == nh - 1)
    def _():
        for ref in (rb_ref, kl_ref, kr_ref):
            clear(ref, 0, 4)

    @pl.when(w == 0)
    def _():
        clear(cl_ref, 0, 8)
        clear(kl_ref, 0, 8)

    @pl.when(w == nw - 1)
    def _():
        clear(cr_ref, 0, 8)
        clear(kr_ref, 0, 8)

    pl.semaphore_wait(bar, count)

    def zcopy():
        return pltpu.make_async_remote_copy(
            src_ref=x_ref, dst_ref=zb_ref, send_sem=zs, recv_sem=zr,
            device_id=(t + 1, h, w), device_id_type=MESH)

    def scopy(i, half):
        dh, dw = SIDES[i]
        rows, lanes = part(dh, dw)
        dst, dlanes = landing(dh, dw)
        src = x_ref if half else zb_ref
        return pltpu.make_async_remote_copy(
            src_ref=src.at[:, rows, lanes], dst_ref=dst.at[pl.ds(4 * half, 4), rows, dlanes],
            send_sem=ss.at[half, i], recv_sem=sr.at[half, i],
            device_id=(t, h + dh, w + dw), device_id_type=MESH)

    @pl.when(t < nt - 1)
    def _():
        zcopy().start()

    for i, side in enumerate(SIDES):
        @pl.when(exists(*side))
        def _():
            scopy(i, 1).start()

    @pl.when(t > 0)
    def _():
        zcopy().wait_recv()
        for i, side in enumerate(SIDES):
            @pl.when(exists(*side))
            def _():
                scopy(i, 0).start()

    for half in (1, 0):
        for i, side in enumerate(SIDES):
            dh, dw = side
            here = exists(-dh, -dw)
            there = exists(dh, dw)
            if half == 0:
                here, there = jnp.logical_and(here, t > 0), jnp.logical_and(there, t > 0)

            @pl.when(here)
            def _():
                scopy(i, half).wait_recv()

            @pl.when(there)
            def _():
                scopy(i, half).wait_send()

    @pl.when(t < nt - 1)
    def _():
        zcopy().wait_send()


def gather_halo(x):
    shapes = [(4, 8, 1536), (8, 8, 1536)] + [(8, 8, 384)] * 4
    vm = pl.BlockSpec(memory_space=pltpu.VMEM)
    return pl.pallas_call(
        halo_kernel,
        out_shape=[jax.ShapeDtypeStruct(s, x.dtype) for s in shapes],
        in_specs=[pl.BlockSpec(memory_space=pl.ANY)],
        out_specs=[vm] * 6,
        scratch_shapes=[
            pltpu.SemaphoreType.DMA, pltpu.SemaphoreType.DMA,
            pltpu.SemaphoreType.DMA((2, 8)), pltpu.SemaphoreType.DMA((2, 8)),
        ],
        compiler_params=pltpu.CompilerParams(collective_id=0, has_side_effects=True),
    )(x)

def activate(v, gain, n):
    meansq = jnp.sum(v * v, axis=-1, keepdims=True) * (1.0 / n)
    half = v * lax.rsqrt(meansq + epsilon) * (0.5 * gain)
    return half + half * jnp.tanh(half)


def take_column(ref, first, col):
    tile, off = divmod(96 * col, 128)
    lane = lax.broadcasted_iota(jnp.int32, (32, 128), 1)

    def lanes(k):
        v = ref[pl.ds(first, 4), :, pl.ds(128 * k, 128)].astype(jnp.float32).reshape(32, 128)
        return pltpu.roll(v, 128 - off, 1) if off else v

    v = lanes(tile)
    if off + 96 > 128:
        v = jnp.where(lane < 128 - off, v, lanes(tile + 1))
    return jnp.where(lane < 96, v, 0.0)


def at(frame, row, col, rows):
    return (frame * rows + row) * 32 + 8 + col


def fill_first(group, blk, rb, cl, cr, kl, kr, gain, S, R):
    f0 = 4 * group

    def put(v, col, rim):
        a = activate(v, gain, 96)
        for k in range(4):
            e = f0 + k
            piece = a[8 * k : 8 * k + 8]
            raw = v[8 * k : 8 * k + 8]
            if rim:
                S[pl.ds(at(e, 10, col, 13), 3, stride=32), :] = piece[0:3]
                S[pl.ds(at(e, 0, col, 13), 2, stride=32), :] = piece[6:8]
            else:
                S[pl.ds(at(e, 2, col, 13), 8, stride=32), :] = piece
            if group == 1 and 0 <= col <= 16:
                if rim:
                    R[pl.ds(at(k, 8, col, 9), 1), :] = raw[0:1]
                else:
                    R[pl.ds(at(k, 0, col, 9), 8, stride=32), :] = raw

    for c in range(16):
        put(take_column(blk, 0, c), c, False)
        put(take_column(rb, f0, c), c, True)
    for c in (-2, -1):
        put(take_column(cl, f0, c + 4), c, False)
        put(take_column(kl, f0, c + 4), c, True)
    for c in (16, 17, 18):
        put(take_column(cr, f0, c - 16), c, False)
        put(take_column(kr, f0, c - 16), c, True)


def build_first(group, S, B1, E1):
    for e in range(4 * group, 4 * group + 4):
        for r in range(13):
            for dc in range(3):
                B1[dc, e, r] = S[pl.ds(at(e, r, dc - 1, 13), 16), :].astype(jnp.bfloat16)
        for dr in range(3):
            for k, c in enumerate((-2, -1, 0, 15, 16, 17, 18)):
                E1[dr, k, e] = S[pl.ds(at(e, dr, c, 13), 16, stride=32), :].astype(jnp.bfloat16)


def conv_first_frames(o, n, B1, E1, W1, gain, Ta, Tb):
    w = W1[...].reshape(27 * 128, 192)
    taps = [(dt, dr, dc) for dt in range(3) for dr in range(3) for dc in range(3)]
    for f in range(o, o + n):
        lhs = [B1[dc, f + dt, pl.ds(dr, 11)].reshape(176, 128) for dt, dr, dc in taps]
        for_ext = [
            jnp.concatenate([E1[dr, k + dc, f + dt] for k in (0, 3, 4)], axis=0) for dt, dr, dc in taps
        ]
        rows = [jnp.concatenate([m, x], axis=0) for m, x in zip(lhs, for_ext)]
        hidden = jnp.dot(jnp.concatenate(rows, axis=1), w, preferred_element_type=jnp.float32)
        second = activate(hidden, gain, 192)
        for r in range(11):
            Ta[pl.ds(at(f, r, 0, 11), 16), :] = second[16 * r : 16 * r + 16, 0:128]
            Tb[pl.ds(at(f, r, 0, 11), 16), 0:64] = second[16 * r : 16 * r + 16, 128:192]
        for k, c in enumerate((-1, 16, 17)):
            m = 176 + 16 * k
            Ta[pl.ds(at(f, 0, c, 11), 11, stride=32), :] = second[m : m + 11, 0:128]
            Tb[pl.ds(at(f, 0, c, 11), 11, stride=32), :] = jnp.concatenate(
                [second[m : m + 11, 128:192], jnp.zeros((11, 64), jnp.float32)], axis=1
            )


def mask_second(o, n, t, h, w, nh, nw, Ta, Tb):
    zero = jnp.zeros((32, 128), jnp.float32)

    def clear(f, r):
        for T in (Ta, Tb):
            T[pl.ds((f * 11 + r) * 32, 32), :] = zero

    @pl.when(h == 0)
    def _():
        for f in range(o, o + n):
            clear(f, 0)

    @pl.when(h == nh - 1)
    def _():
        for f in range(o, o + n):
            clear(f, 9)
            clear(f, 10)

    @pl.when(w == 0)
    def _():
        for f in range(o, o + n):
            for T in (Ta, Tb):
                T[pl.ds(at(f, 0, -1, 11), 11, stride=32), :] = zero[0:11]

    @pl.when(w == nw - 1)
    def _():
        for f in range(o, o + n):
            for T in (Ta, Tb):
                for c in (16, 17):
                    T[pl.ds(at(f, 0, c, 11), 11, stride=32), :] = zero[0:11]

    @pl.when(t == 0)
    def _():
        for f in range(o, min(o + n, 2)):
            for r in range(11):
                clear(f, r)


def build_second(o, n, Ta, Tb, B2, E2):
    for f in range(o, o + n):
        for r in range(11):
            for dc in range(3):
                s = pl.ds(at(f, r, dc - 1, 11), 16)
                B2[dc, f, r, :, 0:128] = Ta[s, :].astype(jnp.bfloat16)
                B2[dc, f, r, :, 128:256] = Tb[s, :].astype(jnp.bfloat16)
        for dr in range(3):
            for k, c in enumerate((15, 16, 17)):
                s = pl.ds(at(f, dr, c, 11), 16, stride=32)
                E2[dr, k, f, :, 0:128] = Ta[s, :].astype(jnp.bfloat16)
                E2[dr, k, f, :, 128:256] = Tb[s, :].astype(jnp.bfloat16)


def conv_second_frames(f, R, B2, E2, W2, WS, Mg):
    taps = [(dt, dr, dc) for dt in range(3) for dr in range(3) for dc in range(3)]
    rows = [
        jnp.concatenate([B2[dc, f + dt, pl.ds(dr, 9)].reshape(144, 256), E2[dr, dc, f + dt]], axis=0)
        for dt, dr, dc in taps
    ]
    raw = jnp.concatenate(
        [R[pl.ds(at(f, r, 0, 9), 16), :].astype(jnp.bfloat16) for r in range(9)]
        + [R[pl.ds(at(f, 0, 16, 9), 16, stride=32), :].astype(jnp.bfloat16)],
        axis=0,
    )
    merged = jnp.dot(
        jnp.concatenate(rows, axis=1), W2[...].reshape(27 * 256, 192), preferred_element_type=jnp.float32
    ) + jnp.dot(raw, WS[...], preferred_element_type=jnp.float32)
    merged = merged.astype(jnp.bfloat16).astype(jnp.float32)
    for r in range(9):
        Mg[0, pl.ds((f * 9 + r) * 32, 16), :] = merged[16 * r : 16 * r + 16, 0:128]
        Mg[1, pl.ds((f * 9 + r) * 32, 16), 0:64] = merged[16 * r : 16 * r + 16, 128:192]
    Mg[0, pl.ds(f * 288 + 16, 9, stride=32), :] = merged[144:153, 0:128]
    Mg[1, pl.ds(f * 288 + 16, 9, stride=32), :] = jnp.concatenate(
        [merged[144:153, 128:192], jnp.zeros((9, 64), jnp.float32)], axis=1
    )


def downscale(h, w, nh, nw, Mg, W3, Q, out_ref):
    zero = jnp.zeros((32, 128), jnp.float32)

    @pl.when(h == nh - 1)
    def _():
        for f in range(4):
            for p in range(2):
                Mg[p, pl.ds((f * 9 + 8) * 32, 32), :] = zero

    @pl.when(w == nw - 1)
    def _():
        for f in range(4):
            for p in range(2):
                Mg[p, pl.ds(f * 288 + 16, 9, stride=32), :] = zero[0:9]

    cols = []
    for dr in range(3):
        for dc in range(3):
            for p in range(2):
                cols.append(jnp.concatenate(
                    [Mg[p, pl.ds((f * 9 + 2 * i + dr) * 32 + dc, 8, stride=2), :]
                     for f in range(4) for i in range(4)], axis=0).astype(jnp.bfloat16))
    res = jnp.dot(
        jnp.concatenate(cols, axis=1), W3[...].reshape(9 * 256, 192), preferred_element_type=jnp.float32
    )
    Q[0] = res[:, 0:128]
    Q[1, :, 0:64] = res[:, 128:192]
    for f in range(4):
        for j in range(8):
            s = pl.ds(f * 32 + j, 4, stride=8)
            out_ref[f, :, 192 * j : 192 * j + 192] = jnp.concatenate(
                [Q[0, s, :], Q[1, s, :][:, 0:64]], axis=1
            ).astype(jnp.bfloat16)


def compute_kernel(x, zb, rb, cl, cr, kl, kr, g1, g2, k1, k2, sc, dw, out_ref,
                   S, R, B1, E1, Ta, Tb, B2, E2, Mg, Q, W1, W2, WS, W3, sem):
    t, h, w = lax.axis_index("tm"), lax.axis_index("height"), lax.axis_index("width")
    nh, nw = lax.axis_size("height"), lax.axis_size("width")
    loads = [
        pltpu.make_async_copy(k1, W1.at[:, pl.ds(0, 96), :], sem.at[0]),
        pltpu.make_async_copy(k2, W2.at[:, pl.ds(0, 192), :], sem.at[1]),
        pltpu.make_async_copy(sc, WS.at[pl.ds(0, 96), :], sem.at[2]),
        pltpu.make_async_copy(dw, W3.at[:, pl.ds(0, 192), :], sem.at[3]),
    ]
    for c in loads:
        c.start()
    W1[:, 96:128, :] = jnp.zeros((27, 32, 192), jnp.bfloat16)
    W2[:, 192:256, :] = jnp.zeros((27, 64, 192), jnp.bfloat16)
    WS[96:128, :] = jnp.zeros((32, 192), jnp.bfloat16)
    W3[:, 192:256, :] = jnp.zeros((9, 64, 192), jnp.bfloat16)
    Tb[...] = jnp.zeros_like(Tb)
    Mg[1] = jnp.zeros(Mg.shape[1:], jnp.float32)
    gain1 = jnp.concatenate([g1[...], jnp.zeros((1, 32), jnp.float32)], axis=1)
    gain2 = g2[...]

    fill_first(1, x, rb, cl, cr, kl, kr, gain1, S, R)
    build_first(1, S, B1, E1)
    loads[0].wait()
    conv_first_frames(4, 2, B1, E1, W1, gain2, Ta, Tb)
    mask_second(4, 2, t, h, w, nh, nw, Ta, Tb)
    build_second(4, 2, Ta, Tb, B2, E2)
    fill_first(0, zb, rb, cl, cr, kl, kr, gain1, S, R)
    build_first(0, S, B1, E1)
    conv_first_frames(0, 4, B1, E1, W1, gain2, Ta, Tb)
    mask_second(0, 4, t, h, w, nh, nw, Ta, Tb)
    build_second(0, 4, Ta, Tb, B2, E2)
    loads[1].wait()
    loads[2].wait()
    for f in range(4):
        conv_second_frames(f, R, B2, E2, W2, WS, Mg)
    loads[3].wait()
    downscale(h, w, nh, nw, Mg, W3, Q, out_ref)


COMPUTE_SCRATCH = [
    pltpu.VMEM(((8 * 13 + 8) * 32, 128), jnp.float32),
    pltpu.VMEM(((4 * 9 + 8) * 32, 128), jnp.float32),
    pltpu.VMEM((3, 8, 13, 16, 128), jnp.bfloat16),
    pltpu.VMEM((3, 7, 8, 16, 128), jnp.bfloat16),
    pltpu.VMEM(((6 * 11 + 8) * 32, 128), jnp.float32),
    pltpu.VMEM(((6 * 11 + 8) * 32, 128), jnp.float32),
    pltpu.VMEM((3, 6, 11, 16, 256), jnp.bfloat16),
    pltpu.VMEM((3, 3, 6, 16, 256), jnp.bfloat16),
    pltpu.VMEM((2, 4 * 9 * 32, 128), jnp.float32),
    pltpu.VMEM((2, 128, 128), jnp.float32),
    pltpu.VMEM((27, 128, 192), jnp.bfloat16),
    pltpu.VMEM((27, 256, 192), jnp.bfloat16),
    pltpu.VMEM((128, 192), jnp.bfloat16),
    pltpu.VMEM((9, 256, 192), jnp.bfloat16),
    pltpu.SemaphoreType.DMA((4,)),
]


def compute(x, halo, g1, g2, k1, k2, sc, dw):
    vm = pl.BlockSpec(memory_space=pltpu.VMEM)
    hbm = pl.BlockSpec(memory_space=pl.ANY)
    return pl.pallas_call(
        compute_kernel,
        out_shape=jax.ShapeDtypeStruct((4, 4, 1536), jnp.bfloat16),
        in_specs=[vm] * 9 + [hbm] * 4,
        out_specs=vm,
        scratch_shapes=COMPUTE_SCRATCH,
        compiler_params=pltpu.CompilerParams(vmem_limit_bytes=56 * 2**20),
    )(x, *halo, g1.reshape(1, 96), g2.reshape(1, 192), k1.reshape(27, 96, 192),
      k2.reshape(27, 192, 192), sc, dw.reshape(9, 192, 192))


def local(x, g1, g2, k1, k2, sc, dw):
    return compute(x, gather_halo(x), g1, g2, k1, k2, sc, dw)


def solution(mesh):
    placed = (P("tm", "height", "width"), P(), P(), P(), P(), P(), P())
    return jax.shard_map(
        local, mesh=mesh, in_specs=placed, out_specs=P("tm", "height", "width"), check_vma=False
    )
```

time: 91.7 us -> 28.1 us (0.31)
  the two profiles are of different devices: /device:TPU:257 before, /device:TPU:33 now
where the time goes in v1:
time: 28.1 us; the launch traced here: 28 us
  Pallas kernels  28 us (100%)
    pallas_call x1, Pallas kernels, gather_halo(): pl.pallas_call(halo_kernel, out_shape=[jax.ShapeDtypeStruct(s, x.dtype) f...  15 us
    pallas_call x1, Pallas kernels, compute(): pl.pallas_call(compute_kernel, out_shape=jax.ShapeDtypeStruct((4, 4, 1536...  13 us

profile of v1, /device:TPU:33, one launch (start us, length us, event | category | flops | bytes accessed | tf_op | source)
XLA Modules:
  0.0 28.0 jit_solution(6303721196698362998)
XLA Ops:
  0.0 15.0 %shard_map.73 = (bf16[4,8,1536]{2,1,0:T(8,128)(2,1)}, bf16[8,8,1536]{2,1,0:T(8,128)(2,1)}, bf16[8,8,384]{2,1,0:T(8,128)(2,1)}, bf16[8,8,384]{2,1,0:T(8,128)(2,1)...) custom-call(bf16[4,8,1536]{2,1,0:T(8,128)(2,1)} %x.1), custom_call_target="tpu_custom_call" | custom-call | tf_op jit(solution)/shard_map/pallas_call | solution.py:144
  15.0 13.0 %shard_map.74 = bf16[4,4,1536]{2,1,0:T(4,128)(2,1)} custom-call(bf16[4,8,1536]{2,1,0:T(8,128)(2,1)} %x.1, bf16[4,8,1536]{2,1,0:T(8,128)(2,1)} %get-tuple-element.11.zb, bf16[8,8,1536]{2,1,0:T(8,128)(2,1)} %get-tuple-element.12.rb, bf16[8,8,384]{2,1,0:T(8,128)(2,1)} %get-tuple-element.13.cl, bf16[8,8,384]{2,1,0:T(8,128)(2,1)} %get-tuple-element.14.cr, ...), custom_call_target="tpu_custom_call" | custom-call | tf_op jit(solution)/shard_map/pallas_call | solution.py:416

commit v2 on v1

v2 whole, which is shorter than its diff:
```python
import functools

import jax
import jax.numpy as jnp
from jax import lax
from jax.experimental import pallas as pl
from jax.experimental.pallas import tpu as pltpu
from jax.sharding import PartitionSpec as P

MESH = pl.DeviceIdType.MESH
epsilon = 1e-06
SIDES = [(-1, 0), (1, 0), (0, -1), (0, 1), (-1, -1), (-1, 1), (1, -1), (1, 1)]


class Halo:
    def __init__(self, x, zb, rb, cl, cr, kl, kr, zs, zr, ss, sr, credit):
        self.x, self.zb, self.rb, self.cl, self.cr, self.kl, self.kr = x, zb, rb, cl, cr, kl, kr
        self.zs, self.zr, self.ss, self.sr, self.credit = zs, zr, ss, sr, credit
        self.t, self.h, self.w = (lax.axis_index(a) for a in ("tm", "height", "width"))
        self.nt, self.nh, self.nw = (lax.axis_size(a) for a in ("tm", "height", "width"))

    def exists(self, dh, dw):
        ok = None
        for pos, by, n in ((self.h, dh, self.nh), (self.w, dw, self.nw)):
            if by:
                one = pos > 0 if by < 0 else pos < n - 1
                ok = one if ok is None else jnp.logical_and(ok, one)
        return ok

    def greet(self):
        t, h, w = self.t, self.h, self.w
        bar = pltpu.get_barrier_semaphore()
        for dh, dw in SIDES:
            @pl.when(self.exists(dh, dw))
            def _():
                pl.semaphore_signal(bar, inc=1, device_id=(t, h + dh, w + dw), device_id_type=MESH)

        @pl.when(t < self.nt - 1)
        def _():
            pl.semaphore_signal(bar, inc=1, device_id=(t + 1, h, w), device_id_type=MESH)

    def clear_outside(self):
        def clear(ref, rows, n):
            ref[:, pl.ds(rows, n), :] = jnp.zeros((8, n, ref.shape[2]), ref.dtype)

        @pl.when(self.t == 0)
        def _():
            self.zb[...] = jnp.zeros_like(self.zb)
            for ref in (self.rb, self.cl, self.cr, self.kl, self.kr):
                ref[pl.ds(0, 4)] = jnp.zeros((4,) + ref.shape[1:], ref.dtype)

        @pl.when(self.h == 0)
        def _():
            for ref in (self.rb, self.kl, self.kr):
                clear(ref, 6, 2)

        @pl.when(self.h == self.nh - 1)
        def _():
            for ref in (self.rb, self.kl, self.kr):
                clear(ref, 0, 4)

        @pl.when(self.w == 0)
        def _():
            clear(self.cl, 0, 8)
            clear(self.kl, 0, 8)

        @pl.when(self.w == self.nw - 1)
        def _():
            clear(self.cr, 0, 8)
            clear(self.kr, 0, 8)

    def meet(self):
        count = (self.t > 0).astype(jnp.int32)
        for side in SIDES:
            count += self.exists(*side).astype(jnp.int32)
        pl.semaphore_wait(pltpu.get_barrier_semaphore(), count)

        @pl.when(self.t > 0)
        def _():
            pl.semaphore_signal(
                self.credit, inc=1, device_id=(self.t - 1, self.h, self.w), device_id_type=MESH)

    def along(self):
        return pltpu.make_async_remote_copy(
            src_ref=self.x, dst_ref=self.zb, send_sem=self.zs, recv_sem=self.zr,
            device_id=(self.t + 1, self.h, self.w), device_id_type=MESH)

    def across(self, i, half):
        dh, dw = SIDES[i]
        rows = {-1: pl.ds(0, 4), 0: pl.ds(0, 8), 1: pl.ds(6, 2)}[dh]
        lanes = {-1: pl.ds(0, 384), 0: pl.ds(0, 1536), 1: pl.ds(1280, 256)}[dw]
        if dw == 0:
            dst = self.rb
        elif dh == 0:
            dst = self.cl if dw == 1 else self.cr
        else:
            dst = self.kl if dw == 1 else self.kr
        src = self.x if half else self.zb
        return pltpu.make_async_remote_copy(
            src_ref=src.at[:, rows, lanes], dst_ref=dst.at[pl.ds(4 * half, 4), rows],
            send_sem=self.ss.at[half, i], recv_sem=self.sr.at[half, i],
            device_id=(self.t, self.h + dh, self.w + dw), device_id_type=MESH)

    def send_across(self, half):
        for i, side in enumerate(SIDES):
            @pl.when(self.exists(*side))
            def _():
                self.across(i, half).start()

    def receive_across(self, half):
        for i, (dh, dw) in enumerate(SIDES):
            @pl.when(self.exists(-dh, -dw))
            def _():
                self.across(i, half).wait_recv()

    def sent_across(self, half):
        for i, side in enumerate(SIDES):
            @pl.when(self.exists(*side))
            def _():
                self.across(i, half).wait_send()

    def send_along(self):
        @pl.when(self.t < self.nt - 1)
        def _():
            pl.semaphore_wait(self.credit, 1)
            self.along().start()

    def relay(self):
        @pl.when(self.t > 0)
        def _():
            self.along().wait_recv()
            self.send_across(0)

    def receive_relayed(self):
        @pl.when(self.t > 0)
        def _():
            self.receive_across(0)

    def finish(self):
        self.sent_across(1)

        @pl.when(self.t > 0)
        def _():
            self.sent_across(0)

        @pl.when(self.t < self.nt - 1)
        def _():
            self.along().wait_send()


def activate(v, gain, n):
    meansq = jnp.sum(v * v, axis=-1, keepdims=True) * (1.0 / n)
    half = v * lax.rsqrt(meansq + epsilon) * (0.5 * gain)
    return half + half * jnp.tanh(half)


def take_column(ref, first, begin):
    tile, off = divmod(begin, 128)
    lane = lax.broadcasted_iota(jnp.int32, (32, 128), 1)

    def lanes(k):
        v = ref[pl.ds(first, 4), :, pl.ds(128 * k, 128)].astype(jnp.float32).reshape(32, 128)
        return pltpu.roll(v, 128 - off, 1) if off else v

    v = lanes(tile)
    if off + 96 > 128:
        v = jnp.where(lane < 128 - off, v, lanes(tile + 1))
    return jnp.where(lane < 96, v, 0.0)


def at(frame, row, col, rows):
    return (frame * rows + row) * 32 + 8 + col


def fill_first(group, part, blk, rb, cl, cr, kl, kr, gain, S, R):
    f0 = 4 * group

    def put(v, col, rim):
        a = activate(v, gain, 96)
        for k in range(4):
            e = f0 + k
            piece = a[8 * k : 8 * k + 8]
            raw = v[8 * k : 8 * k + 8]
            if rim:
                S[pl.ds(at(e, 10, col, 13), 3, stride=32), :] = piece[0:3]
                S[pl.ds(at(e, 0, col, 13), 2, stride=32), :] = piece[6:8]
            else:
                S[pl.ds(at(e, 2, col, 13), 8, stride=32), :] = piece
            if group == 1 and 0 <= col <= 16:
                if rim:
                    R[pl.ds(at(k, 8, col, 9), 1), :] = raw[0:1]
                else:
                    R[pl.ds(at(k, 0, col, 9), 8, stride=32), :] = raw

    if part == "block":
        for c in range(16):
            put(take_column(blk, 0, 96 * c), c, False)
        return
    for c in range(16):
        put(take_column(rb, f0, 96 * c), c, True)
    for c in (-2, -1):
        put(take_column(cl, f0, 64 + 96 * (c + 2)), c, False)
        put(take_column(kl, f0, 64 + 96 * (c + 2)), c, True)
    for c in (16, 17, 18):
        put(take_column(cr, f0, 96 * (c - 16)), c, False)
        put(take_column(kr, f0, 96 * (c - 16)), c, True)


def build_first(group, S, B1, E1):
    for e in range(4 * group, 4 * group + 4):
        for r in range(13):
            for dc in range(3):
                B1[dc, e, r] = S[pl.ds(at(e, r, dc - 1, 13), 16), :].astype(jnp.bfloat16)
        for dr in range(3):
            for k, c in enumerate((-2, -1, 0, 15, 16, 17, 18)):
                E1[dr, k, e] = S[pl.ds(at(e, dr, c, 13), 16, stride=32), :].astype(jnp.bfloat16)


def conv_first_frames(o, n, B1, E1, W1, gain, Ta, Tb):
    w = W1[...].reshape(27 * 128, 192)
    taps = [(dt, dr, dc) for dt in range(3) for dr in range(3) for dc in range(3)]
    for f in range(o, o + n):
        lhs = [B1[dc, f + dt, pl.ds(dr, 11)].reshape(176, 128) for dt, dr, dc in taps]
        for_ext = [
            jnp.concatenate([E1[dr, k + dc, f + dt] for k in (0, 3, 4)], axis=0) for dt, dr, dc in taps
        ]
        rows = [jnp.concatenate([m, x], axis=0) for m, x in zip(lhs, for_ext)]
        hidden = jnp.dot(jnp.concatenate(rows, axis=1), w, preferred_element_type=jnp.float32)
        second = activate(hidden, gain, 192)
        for r in range(11):
            Ta[pl.ds(at(f, r, 0, 11), 16), :] = second[16 * r : 16 * r + 16, 0:128]
            Tb[pl.ds(at(f, r, 0, 11), 16), 0:64] = second[16 * r : 16 * r + 16, 128:192]
        for k, c in enumerate((-1, 16, 17)):
            m = 176 + 16 * k
            Ta[pl.ds(at(f, 0, c, 11), 11, stride=32), :] = second[m : m + 11, 0:128]
            Tb[pl.ds(at(f, 0, c, 11), 11, stride=32), :] = jnp.concatenate(
                [second[m : m + 11, 128:192], jnp.zeros((11, 64), jnp.float32)], axis=1
            )


def mask_second(o, n, t, h, w, nh, nw, Ta, Tb):
    zero = jnp.zeros((32, 128), jnp.float32)

    def clear(f, r):
        for T in (Ta, Tb):
            T[pl.ds((f * 11 + r) * 32, 32), :] = zero

    @pl.when(h == 0)
    def _():
        for f in range(o, o + n):
            clear(f, 0)

    @pl.when(h == nh - 1)
    def _():
        for f in range(o, o + n):
            clear(f, 9)
            clear(f, 10)

    @pl.when(w == 0)
    def _():
        for f in range(o, o + n):
            for T in (Ta, Tb):
                T[pl.ds(at(f, 0, -1, 11), 11, stride=32), :] = zero[0:11]

    @pl.when(w == nw - 1)
    def _():
        for f in range(o, o + n):
            for T in (Ta, Tb):
                for c in (16, 17):
                    T[pl.ds(at(f, 0, c, 11), 11, stride=32), :] = zero[0:11]

    @pl.when(t == 0)
    def _():
        for f in range(o, min(o + n, 2)):
            for r in range(11):
                clear(f, r)


def build_second(o, n, Ta, Tb, B2, E2):
    for f in range(o, o + n):
        for r in range(11):
            for dc in range(3):
                s = pl.ds(at(f, r, dc - 1, 11), 16)
                B2[dc, f, r, :, 0:128] = Ta[s, :].astype(jnp.bfloat16)
                B2[dc, f, r, :, 128:256] = Tb[s, :].astype(jnp.bfloat16)
        for dr in range(3):
            for k, c in enumerate((15, 16, 17)):
                s = pl.ds(at(f, dr, c, 11), 16, stride=32)
                E2[dr, k, f, :, 0:128] = Ta[s, :].astype(jnp.bfloat16)
                E2[dr, k, f, :, 128:256] = Tb[s, :].astype(jnp.bfloat16)


def conv_second_frames(f, R, B2, E2, W2, WS, Mg):
    taps = [(dt, dr, dc) for dt in range(3) for dr in range(3) for dc in range(3)]
    rows = [
        jnp.concatenate([B2[dc, f + dt, pl.ds(dr, 9)].reshape(144, 256), E2[dr, dc, f + dt]], axis=0)
        for dt, dr, dc in taps
    ]
    raw = jnp.concatenate(
        [R[pl.ds(at(f, r, 0, 9), 16), :].astype(jnp.bfloat16) for r in range(9)]
        + [R[pl.ds(at(f, 0, 16, 9), 16, stride=32), :].astype(jnp.bfloat16)],
        axis=0,
    )
    merged = jnp.dot(
        jnp.concatenate(rows, axis=1), W2[...].reshape(27 * 256, 192), preferred_element_type=jnp.float32
    ) + jnp.dot(raw, WS[...], preferred_element_type=jnp.float32)
    merged = merged.astype(jnp.bfloat16).astype(jnp.float32)
    for r in range(9):
        Mg[0, pl.ds((f * 9 + r) * 32, 16), :] = merged[16 * r : 16 * r + 16, 0:128]
        Mg[1, pl.ds((f * 9 + r) * 32, 16), 0:64] = merged[16 * r : 16 * r + 16, 128:192]
    Mg[0, pl.ds(f * 288 + 16, 9, stride=32), :] = merged[144:153, 0:128]
    Mg[1, pl.ds(f * 288 + 16, 9, stride=32), :] = jnp.concatenate(
        [merged[144:153, 128:192], jnp.zeros((9, 64), jnp.float32)], axis=1
    )


def clear_merged(h, w, nh, nw, Mg):
    zero = jnp.zeros((32, 128), jnp.float32)

    @pl.when(h == nh - 1)
    def _():
        for f in range(4):
            for p in range(2):
                Mg[p, pl.ds((f * 9 + 8) * 32, 32), :] = zero

    @pl.when(w == nw - 1)
    def _():
        for f in range(4):
            for p in range(2):
                Mg[p, pl.ds(f * 288 + 16, 9, stride=32), :] = zero[0:9]


def downscale(Mg, W3, Q, out_ref):
    cols = []
    for dr in range(3):
        for dc in range(3):
            for p in range(2):
                cols.append(jnp.concatenate(
                    [Mg[p, pl.ds((f * 9 + 2 * i + dr) * 32 + dc, 8, stride=2), :]
                     for f in range(4) for i in range(4)], axis=0).astype(jnp.bfloat16))
    res = jnp.dot(
        jnp.concatenate(cols, axis=1), W3[...].reshape(9 * 256, 192), preferred_element_type=jnp.float32
    )
    Q[0] = res[:, 0:128]
    Q[1, :, 0:64] = res[:, 128:192]
    for f in range(4):
        for j in range(8):
            s = pl.ds(f * 32 + j, 4, stride=8)
            out_ref[f, :, 192 * j : 192 * j + 192] = jnp.concatenate(
                [Q[0, s, :], Q[1, s, :][:, 0:64]], axis=1
            ).astype(jnp.bfloat16)


def field_kernel(x, g1, g2, k1, k2, sc, k3, out, zb, rb, cl, cr, kl, kr,
                 xs, ga, gb, S, R, B1, E1, Ta, Tb, B2, E2, W1, W2, WS, W3, Mg, Q,
                 sem, zs, zr, ss, sr, credit):
    halo = Halo(x, zb, rb, cl, cr, kl, kr, zs, zr, ss, sr, credit)
    t, h, w, nh, nw = halo.t, halo.h, halo.w, halo.nh, halo.nw
    rims = (rb, cl, cr, kl, kr)
    halo.greet()
    loads = [
        pltpu.make_async_copy(x, xs, sem.at[0]),
        pltpu.make_async_copy(k1, W1.at[:, pl.ds(0, 96), :], sem.at[1]),
        pltpu.make_async_copy(k2, W2.at[:, pl.ds(0, 192), :], sem.at[2]),
        pltpu.make_async_copy(sc, WS.at[pl.ds(0, 96), :], sem.at[3]),
        pltpu.make_async_copy(g1, ga, sem.at[4]),
        pltpu.make_async_copy(g2, gb, sem.at[5]),
        pltpu.make_async_copy(k3, W3.at[:, pl.ds(0, 192), :], sem.at[6]),
    ]
    for c in loads:
        c.start()
    halo.clear_outside()
    halo.meet()
    halo.send_across(1)
    W1[:, 96:128, :] = jnp.zeros((27, 32, 192), jnp.bfloat16)
    W2[:, 192:256, :] = jnp.zeros((27, 64, 192), jnp.bfloat16)
    W3[:, 192:256, :] = jnp.zeros((9, 64, 192), jnp.bfloat16)
    WS[96:128, :] = jnp.zeros((32, 192), jnp.bfloat16)
    Tb[...] = jnp.zeros_like(Tb)
    Mg[1] = jnp.zeros(Mg.shape[1:], jnp.float32)
    loads[0].wait()
    loads[4].wait()
    loads[5].wait()
    gain1 = jnp.concatenate([ga[...], jnp.zeros((1, 32), jnp.float32)], axis=1)
    gain2 = gb[...]
    fill_first(1, "block", xs, *rims, gain1, S, R)
    halo.send_along()
    halo.relay()
    halo.receive_across(1)
    fill_first(1, "rims", xs, *rims, gain1, S, R)
    build_first(1, S, B1, E1)
    loads[1].wait()
    conv_first_frames(4, 2, B1, E1, W1, gain2, Ta, Tb)
    mask_second(4, 2, t, h, w, nh, nw, Ta, Tb)
    build_second(4, 2, Ta, Tb, B2, E2)
    fill_first(0, "block", zb, *rims, gain1, S, R)
    halo.receive_relayed()
    fill_first(0, "rims", zb, *rims, gain1, S, R)
    build_first(0, S, B1, E1)
    conv_first_frames(0, 4, B1, E1, W1, gain2, Ta, Tb)
    mask_second(0, 4, t, h, w, nh, nw, Ta, Tb)
    build_second(0, 4, Ta, Tb, B2, E2)
    loads[2].wait()
    loads[3].wait()
    for f in range(4):
        conv_second_frames(f, R, B2, E2, W2, WS, Mg)
    clear_merged(h, w, nh, nw, Mg)
    loads[6].wait()
    downscale(Mg, W3, Q, out)
    halo.finish()


VM = pl.BlockSpec(memory_space=pltpu.VMEM)
HBM = pl.BlockSpec(memory_space=pltpu.HBM)
LANDING = [(4, 8, 1536), (8, 8, 1536), (8, 8, 256), (8, 8, 384), (8, 8, 256), (8, 8, 384)]


def field(x, g1, g2, k1, k2, sc, k3):
    bf, f32, dma = jnp.bfloat16, jnp.float32, pltpu.SemaphoreType.DMA
    shapes = [
        ((4, 8, 1536), bf), ((1, 96), f32), ((1, 192), f32),
        (((8 * 13 + 8) * 32, 128), f32), (((4 * 9 + 8) * 32, 128), f32),
        ((3, 8, 13, 16, 128), bf), ((3, 7, 8, 16, 128), bf),
        (((6 * 11 + 8) * 32, 128), f32), (((6 * 11 + 8) * 32, 128), f32),
        ((3, 6, 11, 16, 256), bf), ((3, 3, 6, 16, 256), bf),
        ((27, 128, 192), bf), ((27, 256, 192), bf), ((128, 192), bf), ((9, 256, 192), bf),
        ((2, 4 * 9 * 32, 128), f32), ((2, 128, 128), f32),
    ]
    return pl.pallas_call(
        field_kernel,
        out_shape=[jax.ShapeDtypeStruct((4, 4, 1536), bf)] + [jax.ShapeDtypeStruct(s, bf) for s in LANDING],
        in_specs=[HBM] * 7,
        out_specs=[VM] * 7,
        scratch_shapes=[pltpu.VMEM(*s) for s in shapes]
        + [dma((7,)), dma, dma, dma((2, 8)), dma((2, 8)), pltpu.SemaphoreType.REGULAR],
        compiler_params=pltpu.CompilerParams(
            collective_id=0, has_side_effects=True, vmem_limit_bytes=60 * 2**20),
    )(x, g1.reshape(1, 96), g2.reshape(1, 192), k1.reshape(27, 96, 192), k2.reshape(27, 192, 192), sc,
      k3.reshape(9, 192, 192))[0]


def local(x, g1, g2, k1, k2, sc, dw):
    return field(x, g1, g2, k1, k2, sc, dw)


def solution(mesh):
    placed = (P("tm", "height", "width"), P(), P(), P(), P(), P(), P())
    return jax.shard_map(
        local, mesh=mesh, in_specs=placed, out_specs=P("tm", "height", "width"), check_vma=False
    )
```

time: 28.1 us -> 25.4 us (0.904)
  the two profiles are of different devices: /device:TPU:33 before, /device:TPU:1 now
where the time goes in v2:
time: 25.4 us; the launch traced here: 25 us
  Pallas kernels  23.6 us (93%)
  local copies, waits for them, and re-layouts  1.44 us (6%)
    pallas_call x1, Pallas kernels, field(): pl.pallas_call(field_kernel, out_shape=[jax.ShapeDtypeStruct((4, 4, 1536)...  23.6 us
    unnamed x1, local copies, waits for them, and re-layouts  1.44 us

profile of v2, /device:TPU:1, one launch (start us, length us, event | category | flops | bytes accessed | tf_op | source)
XLA Modules:
  0.0 25.0 jit_solution(10357574174671475976)
XLA Ops:
  0.0 23.6 %shard_map.73 = (bf16[4,4,1536]{2,1,0:T(4,128)(2,1)}, bf16[4,8,1536]{2,1,0:T(8,128)(2,1)}, bf16[8,8,1536]{2,1,0:T(8,128)(2,1)}, bf16[8,8,256]{2,1,0:T(8,128)(2,1...) custom-call(bf16[4,8,1536]{2,1,0:T(8,128)(2,1)} %x.1, f32[1,96]{1,0:T(1,128)} %bitcast.9, ...), custom_call_target="tpu_custom_call" | custom-call | tf_op jit(solution)/shard_map/pallas_call | solution.py:429
  23.6 1.4 %copy.9 = bf16[4,4,1536]{2,1,0:T(4,128)(2,1)} copy(bf16[4,4,1536]{2,1,0:T(4,128)(2,1)} %get-tuple-element.6) | data formatting | bytes 98304

commit v3 on v2

--- a/solution.py
+++ b/solution.py
@@ -216,118 +216,127 @@
                 E1[dr, k, e] = S[pl.ds(at(e, dr, c, 13), 16, stride=32), :].astype(jnp.bfloat16)
 
 
-def conv_first_frames(o, n, B1, E1, W1, gain, Ta, Tb):
-    w = W1[...].reshape(27 * 128, 192)
-    taps = [(dt, dr, dc) for dt in range(3) for dr in range(3) for dc in range(3)]
-    for f in range(o, o + n):
-        lhs = [B1[dc, f + dt, pl.ds(dr, 11)].reshape(176, 128) for dt, dr, dc in taps]
-        for_ext = [
-            jnp.concatenate([E1[dr, k + dc, f + dt] for k in (0, 3, 4)], axis=0) for dt, dr, dc in taps
-        ]
-        rows = [jnp.concatenate([m, x], axis=0) for m, x in zip(lhs, for_ext)]
-        hidden = jnp.dot(jnp.concatenate(rows, axis=1), w, preferred_element_type=jnp.float32)
-        second = activate(hidden, gain, 192)
-        for r in range(11):
-            Ta[pl.ds(at(f, r, 0, 11), 16), :] = second[16 * r : 16 * r + 16, 0:128]
-            Tb[pl.ds(at(f, r, 0, 11), 16), 0:64] = second[16 * r : 16 * r + 16, 128:192]
-        for k, c in enumerate((-1, 16, 17)):
-            m = 176 + 16 * k
-            Ta[pl.ds(at(f, 0, c, 11), 11, stride=32), :] = second[m : m + 11, 0:128]
-            Tb[pl.ds(at(f, 0, c, 11), 11, stride=32), :] = jnp.concatenate(
-                [second[m : m + 11, 128:192], jnp.zeros((11, 64), jnp.float32)], axis=1
-            )
-
-
-def mask_second(o, n, t, h, w, nh, nw, Ta, Tb):
-    zero = jnp.zeros((32, 128), jnp.float32)
-
-    def clear(f, r):
-        for T in (Ta, Tb):
-            T[pl.ds((f * 11 + r) * 32, 32), :] = zero
-
-    @pl.when(h == 0)
-    def _():
-        for f in range(o, o + n):
-            clear(f, 0)
-
-    @pl.when(h == nh - 1)
-    def _():
-        for f in range(o, o + n):
-            clear(f, 9)
-            clear(f, 10)
-
-    @pl.when(w == 0)
-    def _():
-        for f in range(o, o + n):
-            for T in (Ta, Tb):
-                T[pl.ds(at(f, 0, -1, 11), 11, stride=32), :] = zero[0:11]
-
-    @pl.when(w == nw - 1)
-    def _():
-        for f in range(o, o + n):
-            for T in (Ta, Tb):
-                for c in (16, 17):
-                    T[pl.ds(at(f, 0, c, 11), 11, stride=32), :] = zero[0:11]
-
-    @pl.when(t == 0)
-    def _():
-        for f in range(o, min(o + n, 2)):
-            for r in range(11):
-                clear(f, r)
-
-
-def build_second(o, n, Ta, Tb, B2, E2):
-    for f in range(o, o + n):
-        for r in range(11):
-            for dc in range(3):
-                s = pl.ds(at(f, r, dc - 1, 11), 16)
-                B2[dc, f, r, :, 0:128] = Ta[s, :].astype(jnp.bfloat16)
-                B2[dc, f, r, :, 128:256] = Tb[s, :].astype(jnp.bfloat16)
-        for dr in range(3):
-            for k, c in enumerate((15, 16, 17)):
-                s = pl.ds(at(f, dr, c, 11), 16, stride=32)
-                E2[dr, k, f, :, 0:128] = Ta[s, :].astype(jnp.bfloat16)
-                E2[dr, k, f, :, 128:256] = Tb[s, :].astype(jnp.bfloat16)
-
-
-def conv_second_frames(f, R, B2, E2, W2, WS, Mg):
-    taps = [(dt, dr, dc) for dt in range(3) for dr in range(3) for dc in range(3)]
+TAPS = [(dr, dc) for dr in range(3) for dc in range(3)]
+
+
+class Keep:
+    def __init__(self, h, w, nh, nw):
+        f32 = jnp.float32
+        self.top, self.bottom = (h > 0).astype(f32), (h < nh - 1).astype(f32)
+        self.left, self.right = (w > 0).astype(f32), (w < nw - 1).astype(f32)
+
+    def rows(self, first_below, top):
+        row = lax.broadcasted_iota(jnp.int32, (16, 128), 0)
+        m = jnp.where(row >= first_below, self.bottom, 1.0)
+        return jnp.where(row == 0, self.top, m) if top else m
+
+
+def conv_first(o, lo, hi, B1, E1, W1):
     rows = [
-        jnp.concatenate([B2[dc, f + dt, pl.ds(dr, 9)].reshape(144, 256), E2[dr, dc, f + dt]], axis=0)
-        for dt, dr, dc in taps
+        jnp.concatenate(
+            [B1[dc, o + dt, pl.ds(dr, 11)].reshape(176, 128)] + [E1[dr, k + dc, o + dt] for k in (0, 3, 4)], axis=0)
+        for dt in range(lo, hi) for dr, dc in TAPS
     ]
-    raw = jnp.concatenate(
-        [R[pl.ds(at(f, r, 0, 9), 16), :].astype(jnp.bfloat16) for r in range(9)]
-        + [R[pl.ds(at(f, 0, 16, 9), 16, stride=32), :].astype(jnp.bfloat16)],
-        axis=0,
-    )
-    merged = jnp.dot(
-        jnp.concatenate(rows, axis=1), W2[...].reshape(27 * 256, 192), preferred_element_type=jnp.float32
-    ) + jnp.dot(raw, WS[...], preferred_element_type=jnp.float32)
+    w = W1[pl.ds(9 * lo, 9 * (hi - lo))].reshape((hi - lo) * 9 * 128, 192)
+    return jnp.dot(jnp.concatenate(rows, axis=1), w, preferred_element_type=jnp.float32)
+
+
+def put_second(f, hidden, gain, keep, Ta, Tb):
+    second = activate(hidden, gain, 192)
+    pa = second[:, 0:128]
+    pb = jnp.concatenate([second[:, 128:192], second[:, 128:192]], axis=1)
+    for r in range(11):
+        for T, p in ((Ta, pa), (Tb, pb)):
+            v = p[16 * r : 16 * r + 16]
+            if r == 0:
+                v = v * keep.top
+            if r >= 9:
+                v = v * keep.bottom
+            T[pl.ds(at(f, r, 0, 11), 16), :] = v
+    inside = keep.rows(9, True)
+    for k, c in enumerate((-1, 16, 17)):
+        m = 176 + 16 * k
+        side = inside * (keep.left if k == 0 else keep.right)
+        for T, p in ((Ta, pa), (Tb, pb)):
+            T[pl.ds(at(f, 0, c, 11), 11, stride=32), :] = (p[m : m + 16] * side)[0:11]
+
+
+def halves(a, b):
+    lane = lax.broadcasted_iota(jnp.int32, a.shape, 1)
+    return jnp.where(lane < 64, a, b).astype(jnp.bfloat16)
+
+
+def build_second(f, Ta, Tb, A2, P01, P2r, D2, A2e, P01e, P2re, D2e):
+    for r in range(11):
+        spans = [pl.ds(at(f, r, dc - 1, 11), 16) for dc in range(3)]
+        for dc in range(3):
+            A2[dc, f, r] = Ta[spans[dc], :].astype(jnp.bfloat16)
+        P01[f, r] = halves(Tb[spans[0], :], Tb[spans[1], :])
+        if r < 9:
+            P2r[f, r] = halves(Tb[spans[2], :], Tb[pl.ds(at(f, r + 1, 1, 11), 16), :])
+        if r >= 2:
+            D2[f, r - 2] = Tb[spans[2], :].astype(jnp.bfloat16)
+    for dr in range(3):
+        spans = [pl.ds(at(f, dr, c, 11), 16, stride=32) for c in (15, 16, 17)]
+        for k in range(3):
+            A2e[dr, k, f] = Ta[spans[k], :].astype(jnp.bfloat16)
+        P01e[dr, f] = halves(Tb[spans[0], :], Tb[spans[1], :])
+    rows = [Tb[pl.ds(at(f, dr, 17, 11), 16, stride=32), :] for dr in range(3)]
+    P2re[f] = halves(rows[0], rows[1])
+    D2e[f] = rows[2].astype(jnp.bfloat16)
+
+
+def build_pair(f, Tb, P2f, P2fe):
+    for r in range(2, 11):
+        P2f[f, r - 2] = halves(Tb[pl.ds(at(f, r, 1, 11), 16), :], Tb[pl.ds(at(f + 1, r, 1, 11), 16), :])
+    P2fe[f] = halves(*(Tb[pl.ds(at(g, 2, 17, 11), 16, stride=32), :] for g in (f, f + 1)))
+
+
+BASE = (0, 14, 27)
+
+
+def tile_of(dt, dr, dc):
+    if dc < 2:
+        return BASE[dt] + 9 + dr, dc
+    if dr < 2:
+        return BASE[dt] + 12, dr
+    return (13, dt) if dt < 2 else (40, 0)
+
+
+def conv_second(f, first, last, ops, W2):
+    A2, P01, P2r, D2, A2e, P01e, P2re, D2e, P2f, P2fe, R = ops
+
+    def tile(i):
+        if i == 41:
+            return [R[pl.ds(at(f, r, 0, 9), 16), :].astype(jnp.bfloat16) for r in range(9)] + [
+                R[pl.ds(at(f, 0, 16, 9), 16, stride=32), :].astype(jnp.bfloat16)]
+        if i == 13:
+            return [P2f[f].reshape(144, 128), P2fe[f]]
+        if i == 40:
+            return [D2[f + 2].reshape(144, 128), D2e[f + 2]]
+        dt = 2 if i >= BASE[2] else 1 if i >= BASE[1] else 0
+        k, g = i - BASE[dt], f + dt
+        if k < 9:
+            dr, dc = TAPS[k]
+            return [A2[dc, g, pl.ds(dr, 9)].reshape(144, 128), A2e[dr, dc, g]]
+        if k < 12:
+            return [P01[g, pl.ds(k - 9, 9)].reshape(144, 128), P01e[k - 9, g]]
+        return [P2r[g].reshape(144, 128), P2re[g]]
+
+    lhs = jnp.concatenate([jnp.concatenate(tile(i), axis=0) for i in range(first, last)], axis=1)
+    w = W2[pl.ds(first, last - first)].reshape((last - first) * 128, 192)
+    return jnp.dot(lhs, w, preferred_element_type=jnp.float32)
+
+
+def put_merged(f, merged, keep, Mg):
     merged = merged.astype(jnp.bfloat16).astype(jnp.float32)
-    for r in range(9):
-        Mg[0, pl.ds((f * 9 + r) * 32, 16), :] = merged[16 * r : 16 * r + 16, 0:128]
-        Mg[1, pl.ds((f * 9 + r) * 32, 16), 0:64] = merged[16 * r : 16 * r + 16, 128:192]
-    Mg[0, pl.ds(f * 288 + 16, 9, stride=32), :] = merged[144:153, 0:128]
-    Mg[1, pl.ds(f * 288 + 16, 9, stride=32), :] = jnp.concatenate(
-        [merged[144:153, 128:192], jnp.zeros((9, 64), jnp.float32)], axis=1
-    )
-
-
-def clear_merged(h, w, nh, nw, Mg):
-    zero = jnp.zeros((32, 128), jnp.float32)
-
-    @pl.when(h == nh - 1)
-    def _():
-        for f in range(4):
-            for p in range(2):
-                Mg[p, pl.ds((f * 9 + 8) * 32, 32), :] = zero
-
-    @pl.when(w == nw - 1)
-    def _():
-        for f in range(4):
-            for p in range(2):
-                Mg[p, pl.ds(f * 288 + 16, 9, stride=32), :] = zero[0:9]
+    pb = jnp.concatenate([merged[:, 128:192], jnp.zeros((160, 64), jnp.float32)], axis=1)
+    side = keep.rows(8, False) * keep.right
+    for p, v in enumerate((merged[:, 0:128], pb)):
+        for r in range(9):
+            part = v[16 * r : 16 * r + 16]
+            Mg[p, pl.ds((f * 9 + r) * 32, 16), :] = part * keep.bottom if r == 8 else part
+        Mg[p, pl.ds(f * 288 + 16, 9, stride=32), :] = (v[144:160] * side)[0:9]
 
 
 def downscale(Mg, W3, Q, out_ref):
@@ -352,60 +361,86 @@
 
 
 def field_kernel(x, g1, g2, k1, k2, sc, k3, out, zb, rb, cl, cr, kl, kr,
-                 xs, ga, gb, S, R, B1, E1, Ta, Tb, B2, E2, W1, W2, WS, W3, Mg, Q,
-                 sem, zs, zr, ss, sr, credit):
+                 xs, ga, gb, S, R, B1, E1, Ta, Tb, A2, P01, P2r, D2, A2e, P01e, P2re, D2e, P2f, P2fe,
+                 W1, W2, W3, Mg, Q, acc1, acc2, sem, wsem, zs, zr, ss, sr, credit):
     halo = Halo(x, zb, rb, cl, cr, kl, kr, zs, zr, ss, sr, credit)
-    t, h, w, nh, nw = halo.t, halo.h, halo.w, halo.nh, halo.nw
     rims = (rb, cl, cr, kl, kr)
     halo.greet()
     loads = [
         pltpu.make_async_copy(x, xs, sem.at[0]),
-        pltpu.make_async_copy(k1, W1.at[:, pl.ds(0, 96), :], sem.at[1]),
-        pltpu.make_async_copy(k2, W2.at[:, pl.ds(0, 192), :], sem.at[2]),
-        pltpu.make_async_copy(sc, WS.at[pl.ds(0, 96), :], sem.at[3]),
-        pltpu.make_async_copy(g1, ga, sem.at[4]),
-        pltpu.make_async_copy(g2, gb, sem.at[5]),
-        pltpu.make_async_copy(k3, W3.at[:, pl.ds(0, 192), :], sem.at[6]),
+        pltpu.make_async_copy(g1, ga, sem.at[1]),
+        pltpu.make_async_copy(g2, gb, sem.at[2]),
+        pltpu.make_async_copy(k1, W1.at[:, pl.ds(0, 96), :], sem.at[3]),
+        pltpu.make_async_copy(k3, W3.at[:, pl.ds(0, 192), :], sem.at[4]),
     ]
+    loads2 = [pltpu.make_async_copy(sc, W2.at[41, pl.ds(0, 96), :], wsem.at[30])]
+    for dt in range(3):
+        loads2.append(pltpu.make_async_copy(
+            k2.at[pl.ds(9 * dt, 9), pl.ds(0, 128), :], W2.at[pl.ds(BASE[dt], 9)], wsem.at[27 + dt]))
+        for n, (dr, dc) in enumerate(TAPS):
+            i, half = tile_of(dt, dr, dc)
+            loads2.append(pltpu.make_async_copy(
+                k2.at[9 * dt + n, pl.ds(128, 64), :], W2.at[i, pl.ds(64 * half, 64), :], wsem.at[9 * dt + n]))
     for c in loads:
         c.start()
     halo.clear_outside()
     halo.meet()
     halo.send_across(1)
+    for c in loads2:
+        c.start()
     W1[:, 96:128, :] = jnp.zeros((27, 32, 192), jnp.bfloat16)
-    W2[:, 192:256, :] = jnp.zeros((27, 64, 192), jnp.bfloat16)
+    W2[40, 64:128, :] = jnp.zeros((64, 192), jnp.bfloat16)
+    W2[41, 96:128, :] = jnp.zeros((32, 192), jnp.bfloat16)
     W3[:, 192:256, :] = jnp.zeros((9, 64, 192), jnp.bfloat16)
-    WS[96:128, :] = jnp.zeros((32, 192), jnp.bfloat16)
-    Tb[...] = jnp.zeros_like(Tb)
     Mg[1] = jnp.zeros(Mg.shape[1:], jnp.float32)
-    loads[0].wait()
-    loads[4].wait()
-    loads[5].wait()
+    for c in loads[:3]:
+        c.wait()
     gain1 = jnp.concatenate([ga[...], jnp.zeros((1, 32), jnp.float32)], axis=1)
     gain2 = gb[...]
+    keep = Keep(halo.h, halo.w, halo.nh, halo.nw)
+    ops = (A2, P01, P2r, D2, A2e, P01e, P2re, D2e)
+    all_ops = ops + (P2f, P2fe, R)
+
     fill_first(1, "block", xs, *rims, gain1, S, R)
     halo.send_along()
     halo.relay()
     halo.receive_across(1)
+    loads[3].wait()
     fill_first(1, "rims", xs, *rims, gain1, S, R)
     build_first(1, S, B1, E1)
-    loads[1].wait()
-    conv_first_frames(4, 2, B1, E1, W1, gain2, Ta, Tb)
-    mask_second(4, 2, t, h, w, nh, nw, Ta, Tb)
-    build_second(4, 2, Ta, Tb, B2, E2)
+    for o in (4, 5):
+        put_second(o, conv_first(o, 0, 3, B1, E1, W1), gain2, keep, Ta, Tb)
     fill_first(0, "block", zb, *rims, gain1, S, R)
+    acc1[0] = conv_first(2, 2, 3, B1, E1, W1)
+    acc1[1] = conv_first(3, 1, 3, B1, E1, W1)
+    for o in (4, 5):
+        build_second(o, Ta, Tb, *ops)
+    for c in loads2:
+        c.wait()
+    acc2[0] = conv_second(2, 27, 42, all_ops, W2)
+    acc2[1] = conv_second(3, 14, 42, all_ops, W2)
+    loads[4].wait()
     halo.receive_relayed()
+
     fill_first(0, "rims", zb, *rims, gain1, S, R)
     build_first(0, S, B1, E1)
-    conv_first_frames(0, 4, B1, E1, W1, gain2, Ta, Tb)
-    mask_second(0, 4, t, h, w, nh, nw, Ta, Tb)
-    build_second(0, 4, Ta, Tb, B2, E2)
-    loads[2].wait()
-    loads[3].wait()
-    for f in range(4):
-        conv_second_frames(f, R, B2, E2, W2, WS, Mg)
-    clear_merged(h, w, nh, nw, Mg)
-    loads[6].wait()
+    for o in (3, 2, 1, 0):
+        if o == 3:
+            hidden = acc1[1] + conv_first(3, 0, 1, B1, E1, W1)
+        elif o == 2:
+            hidden = acc1[0] + conv_first(2, 0, 2, B1, E1, W1)
+        else:
+            hidden = conv_first(o, 0, 3, B1, E1, W1)
+        put_second(o, hidden, gain2, keep, Ta, Tb)
+        build_second(o, Ta, Tb, *ops)
+        build_pair(o, Tb, P2f, P2fe)
+        if o == 3:
+            merged = acc2[1] + conv_second(3, 0, 14, all_ops, W2)
+        elif o == 2:
+            merged = acc2[0] + conv_second(2, 0, 27, all_ops, W2)
+        else:
+            merged = conv_second(o, 0, 42, all_ops, W2)
+        put_merged(o, merged, keep, Mg)
     downscale(Mg, W3, Q, out)
     halo.finish()
 
@@ -422,9 +457,11 @@
         (((8 * 13 + 8) * 32, 128), f32), (((4 * 9 + 8) * 32, 128), f32),
         ((3, 8, 13, 16, 128), bf), ((3, 7, 8, 16, 128), bf),
         (((6 * 11 + 8) * 32, 128), f32), (((6 * 11 + 8) * 32, 128), f32),
-        ((3, 6, 11, 16, 256), bf), ((3, 3, 6, 16, 256), bf),
-        ((27, 128, 192), bf), ((27, 256, 192), bf), ((128, 192), bf), ((9, 256, 192), bf),
-        ((2, 4 * 9 * 32, 128), f32), ((2, 128, 128), f32),
+        ((3, 6, 11, 16, 128), bf), ((6, 11, 16, 128), bf), ((6, 9, 16, 128), bf), ((6, 9, 16, 128), bf),
+        ((3, 3, 6, 16, 128), bf), ((3, 6, 16, 128), bf), ((6, 16, 128), bf), ((6, 16, 128), bf),
+        ((4, 9, 16, 128), bf), ((4, 16, 128), bf),
+        ((27, 128, 192), bf), ((42, 128, 192), bf), ((9, 256, 192), bf),
+        ((2, 4 * 9 * 32, 128), f32), ((2, 128, 128), f32), ((2, 224, 192), f32), ((2, 160, 192), f32),
     ]
     return pl.pallas_call(
         field_kernel,
@@ -432,15 +469,15 @@
         in_specs=[HBM] * 7,
         out_specs=[VM] * 7,
         scratch_shapes=[pltpu.VMEM(*s) for s in shapes]
-        + [dma((7,)), dma, dma, dma((2, 8)), dma((2, 8)), pltpu.SemaphoreType.REGULAR],
+        + [dma((5,)), dma((31,)), dma, dma, dma((2, 8)), dma((2, 8)), pltpu.SemaphoreType.REGULAR],
         compiler_params=pltpu.CompilerParams(
-            collective_id=0, has_side_effects=True, vmem_limit_bytes=60 * 2**20),
-    )(x, g1.reshape(1, 96), g2.reshape(1, 192), k1.reshape(27, 96, 192), k2.reshape(27, 192, 192), sc,
-      k3.reshape(9, 192, 192))[0]
+            collective_id=0, has_side_effects=True, vmem_limit_bytes=40 * 2**20),
+    )(x, g1, g2, k1, k2, sc, k3)[0]
 
 
 def local(x, g1, g2, k1, k2, sc, dw):
-    return field(x, g1, g2, k1, k2, sc, dw)
+    keep = [pltpu.with_memory_space_constraint(a, pltpu.HBM) for a in (x, g1.reshape(1, 96), g2.reshape(1, 192), k1.reshape(27, 96, 192), k2.reshape(27, 192, 192), sc, dw.reshape(9, 192, 192))]
+    return field(*keep)
 
 
 def solution(mesh):

time: 25.4 us -> 22 us (0.87)
  Pallas kernels: 23.6 us -> 21.2 us
  local copies, waits for them, and re-layouts: 1.44 us -> 0.62 us
    pallas_call x1, Pallas kernels: 23.6 us -> 21.2 us  [field(): pl.pallas_call(field_kernel, out_shape=[jax.ShapeDtypeStruct((4, 4, 1536)...]
    unnamed x1, local copies, waits for them, and re-layouts: 1.44 us -> 0.62 us
where the time goes in v3:
time: 22 us; the launch traced here: 21.8 us
  Pallas kernels  21.2 us (96%)
  local copies, waits for them, and re-layouts  0.62 us (3%)
    pallas_call x1, Pallas kernels, field(): pl.pallas_call(field_kernel, out_shape=[jax.ShapeDtypeStruct((4, 4, 1536)...  21.2 us
    unnamed x1, local copies, waits for them, and re-layouts  0.62 us

profile of v3, /device:TPU:1, one launch (start us, length us, event | category | flops | bytes accessed | tf_op | source)
XLA Modules:
  0.0 21.8 jit_solution(7248006794736589616)
XLA Ops:
  0.0 21.2 %shard_map.73 = (bf16[4,4,1536]{2,1,0:T(4,128)(2,1)S(1)}, bf16[4,8,1536]{2,1,0:T(8,128)(2,1)}, bf16[8,8,1536]{2,1,0:T(8,128)(2,1)}, bf16[8,8,256]{2,1,0:T(8,128)...) custom-call(bf16[4,8,1536]{2,1,0:T(8,128)(2,1)} %x.1, f32[1,96]{1,0:T(1,128)} %bitcast.9, ...), custom_call_target="tpu_custom_call" | custom-call | tf_op jit(solution)/shard_map/pallas_call | solution.py:466
  21.2 0.6 %copy.9 = bf16[4,4,1536]{2,1,0:T(4,128)(2,1)} copy(bf16[4,4,1536]{2,1,0:T(4,128)(2,1)S(1)} %get-tuple-element.6) | data formatting | bytes 98304

commit v4 on v3

--- a/solution.py
+++ b/solution.py
@@ -10,6 +10,8 @@
 MESH = pl.DeviceIdType.MESH
 epsilon = 1e-06
 SIDES = [(-1, 0), (1, 0), (0, -1), (0, 1), (-1, -1), (-1, 1), (1, -1), (1, 1)]
+
+BATCH = [(4, 4), (2, 2), (0, 2)]
 
 
 class Halo:
@@ -80,12 +82,14 @@
             pl.semaphore_signal(
                 self.credit, inc=1, device_id=(self.t - 1, self.h, self.w), device_id_type=MESH)
 
-    def along(self):
+    def along(self, batch):
+        frames = pl.ds(BATCH[batch][0], 2)
         return pltpu.make_async_remote_copy(
-            src_ref=self.x, dst_ref=self.zb, send_sem=self.zs, recv_sem=self.zr,
+            src_ref=self.x.at[frames], dst_ref=self.zb.at[frames],
+            send_sem=self.zs.at[batch], recv_sem=self.zr.at[batch],
             device_id=(self.t + 1, self.h, self.w), device_id_type=MESH)
 
-    def across(self, i, half):
+    def across(self, i, batch):
         dh, dw = SIDES[i]
         rows = {-1: pl.ds(0, 4), 0: pl.ds(0, 8), 1: pl.ds(6, 2)}[dh]
         lanes = {-1: pl.ds(0, 384), 0: pl.ds(0, 1536), 1: pl.ds(1280, 256)}[dw]
@@ -95,57 +99,61 @@
             dst = self.cl if dw == 1 else self.cr
         else:
             dst = self.kl if dw == 1 else self.kr
-        src = self.x if half else self.zb
+        first, n = BATCH[batch]
+        src = self.zb.at[pl.ds(first, n), rows, lanes] if batch else self.x.at[:, rows, lanes]
         return pltpu.make_async_remote_copy(
-            src_ref=src.at[:, rows, lanes], dst_ref=dst.at[pl.ds(4 * half, 4), rows],
-            send_sem=self.ss.at[half, i], recv_sem=self.sr.at[half, i],
+            src_ref=src, dst_ref=dst.at[pl.ds(first, n), rows],
+            send_sem=self.ss.at[batch, i], recv_sem=self.sr.at[batch, i],
             device_id=(self.t, self.h + dh, self.w + dw), device_id_type=MESH)
 
-    def send_across(self, half):
+    def send_across(self, batch):
         for i, side in enumerate(SIDES):
             @pl.when(self.exists(*side))
             def _():
-                self.across(i, half).start()
-
-    def receive_across(self, half):
+                self.across(i, batch).start()
+
+    def receive_across(self, batch):
         for i, (dh, dw) in enumerate(SIDES):
             @pl.when(self.exists(-dh, -dw))
             def _():
-                self.across(i, half).wait_recv()
-
-    def sent_across(self, half):
+                self.across(i, batch).wait_recv()
+
+    def sent_across(self, batch):
         for i, side in enumerate(SIDES):
             @pl.when(self.exists(*side))
             def _():
-                self.across(i, half).wait_send()
+                self.across(i, batch).wait_send()
 
     def send_along(self):
         @pl.when(self.t < self.nt - 1)
         def _():
             pl.semaphore_wait(self.credit, 1)
-            self.along().start()
-
-    def relay(self):
+            self.along(1).start()
+            self.along(2).start()
+
+    def relay(self, batch):
         @pl.when(self.t > 0)
         def _():
-            self.along().wait_recv()
-            self.send_across(0)
-
-    def receive_relayed(self):
+            self.along(batch).wait_recv()
+            self.send_across(batch)
+
+    def receive_relayed(self, batch):
         @pl.when(self.t > 0)
         def _():
-            self.receive_across(0)
+            self.receive_across(batch)
 
     def finish(self):
-        self.sent_across(1)
+        self.sent_across(0)
 
         @pl.when(self.t > 0)
         def _():
-            self.sent_across(0)
+            self.sent_across(1)
+            self.sent_across(2)
 
         @pl.when(self.t < self.nt - 1)
         def _():
-            self.along().wait_send()
+            self.along(1).wait_send()
+            self.along(2).wait_send()
 
 
 def activate(v, gain, n):
@@ -154,12 +162,12 @@
     return half + half * jnp.tanh(half)
 
 
-def take_column(ref, first, begin):
+def take_column(ref, first, n, begin):
     tile, off = divmod(begin, 128)
-    lane = lax.broadcasted_iota(jnp.int32, (32, 128), 1)
+    lane = lax.broadcasted_iota(jnp.int32, (8 * n, 128), 1)
 
     def lanes(k):
-        v = ref[pl.ds(first, 4), :, pl.ds(128 * k, 128)].astype(jnp.float32).reshape(32, 128)
+        v = ref[pl.ds(first, n), :, pl.ds(128 * k, 128)].astype(jnp.float32).reshape(8 * n, 128)
         return pltpu.roll(v, 128 - off, 1) if off else v
 
     v = lanes(tile)
@@ -172,12 +180,10 @@
     return (frame * rows + row) * 32 + 8 + col
 
 
-def fill_first(group, part, blk, rb, cl, cr, kl, kr, gain, S, R):
-    f0 = 4 * group
-
+def fill_first(f0, n, part, blk, rb, cl, cr, kl, kr, gain, S, R):
     def put(v, col, rim):
         a = activate(v, gain, 96)
-        for k in range(4):
+        for k in range(n):
             e = f0 + k
             piece = a[8 * k : 8 * k + 8]
             raw = v[8 * k : 8 * k + 8]
@@ -186,28 +192,28 @@
                 S[pl.ds(at(e, 0, col, 13), 2, stride=32), :] = piece[6:8]
             else:
                 S[pl.ds(at(e, 2, col, 13), 8, stride=32), :] = piece
-            if group == 1 and 0 <= col <= 16:
+            if e >= 4 and 0 <= col <= 16:
                 if rim:
-                    R[pl.ds(at(k, 8, col, 9), 1), :] = raw[0:1]
+                    R[pl.ds(at(e - 4, 8, col, 9), 1), :] = raw[0:1]
                 else:
-                    R[pl.ds(at(k, 0, col, 9), 8, stride=32), :] = raw
+                    R[pl.ds(at(e - 4, 0, col, 9), 8, stride=32), :] = raw
 
     if part == "block":
         for c in range(16):
-            put(take_column(blk, 0, 96 * c), c, False)
+            put(take_column(blk, 0, n, 96 * c), c, False)
         return
     for c in range(16):
-        put(take_column(rb, f0, 96 * c), c, True)
+        put(take_column(rb, f0, n, 96 * c), c, True)
     for c in (-2, -1):
-        put(take_column(cl, f0, 64 + 96 * (c + 2)), c, False)
-        put(take_column(kl, f0, 64 + 96 * (c + 2)), c, True)
+        put(take_column(cl, f0, n, 64 + 96 * (c + 2)), c, False)
+        put(take_column(kl, f0, n, 64 + 96 * (c + 2)), c, True)
     for c in (16, 17, 18):
-        put(take_column(cr, f0, 96 * (c - 16)), c, False)
-        put(take_column(kr, f0, 96 * (c - 16)), c, True)
-
-
-def build_first(group, S, B1, E1):
-    for e in range(4 * group, 4 * group + 4):
+        put(take_column(cr, f0, n, 96 * (c - 16)), c, False)
+        put(take_column(kr, f0, n, 96 * (c - 16)), c, True)
+
+
+def build_first(f0, n, S, B1, E1):
+    for e in range(f0, f0 + n):
         for r in range(13):
             for dc in range(3):
                 B1[dc, e, r] = S[pl.ds(at(e, r, dc - 1, 13), 16), :].astype(jnp.bfloat16)
@@ -339,20 +345,20 @@
         Mg[p, pl.ds(f * 288 + 16, 9, stride=32), :] = (v[144:160] * side)[0:9]
 
 
-def downscale(Mg, W3, Q, out_ref):
+def downscale(f0, n, Mg, W3, Q, out_ref):
     cols = []
     for dr in range(3):
         for dc in range(3):
             for p in range(2):
                 cols.append(jnp.concatenate(
                     [Mg[p, pl.ds((f * 9 + 2 * i + dr) * 32 + dc, 8, stride=2), :]
-                     for f in range(4) for i in range(4)], axis=0).astype(jnp.bfloat16))
+                     for f in range(f0, f0 + n) for i in range(4)], axis=0).astype(jnp.bfloat16))
     res = jnp.dot(
         jnp.concatenate(cols, axis=1), W3[...].reshape(9 * 256, 192), preferred_element_type=jnp.float32
     )
-    Q[0] = res[:, 0:128]
-    Q[1, :, 0:64] = res[:, 128:192]
-    for f in range(4):
+    Q[0, pl.ds(32 * f0, 32 * n)] = res[:, 0:128]
+    Q[1, pl.ds(32 * f0, 32 * n), 0:64] = res[:, 128:192]
+    for f in range(f0, f0 + n):
         for j in range(8):
             s = pl.ds(f * 32 + j, 4, stride=8)
             out_ref[f, :, 192 * j : 192 * j + 192] = jnp.concatenate(
@@ -360,8 +366,8 @@
             ).astype(jnp.bfloat16)
 
 
-def field_kernel(x, g1, g2, k1, k2, sc, k3, out, zb, rb, cl, cr, kl, kr,
-                 xs, ga, gb, S, R, B1, E1, Ta, Tb, A2, P01, P2r, D2, A2e, P01e, P2re, D2e, P2f, P2fe,
+def field_kernel(x, g1, g2, k1, k2, sc, k3, out,
+                 zb, rb, cl, cr, kl, kr, xs, ga, gb, S, R, B1, E1, Ta, Tb, A2, P01, P2r, D2, A2e, P01e, P2re, D2e, P2f, P2fe,
                  W1, W2, W3, Mg, Q, acc1, acc2, sem, wsem, zs, zr, ss, sr, credit):
     halo = Halo(x, zb, rb, cl, cr, kl, kr, zs, zr, ss, sr, credit)
     rims = (rb, cl, cr, kl, kr)
@@ -385,7 +391,7 @@
         c.start()
     halo.clear_outside()
     halo.meet()
-    halo.send_across(1)
+    halo.send_across(0)
     for c in loads2:
         c.start()
     W1[:, 96:128, :] = jnp.zeros((27, 32, 192), jnp.bfloat16)
@@ -401,47 +407,52 @@
     ops = (A2, P01, P2r, D2, A2e, P01e, P2re, D2e)
     all_ops = ops + (P2f, P2fe, R)
 
-    fill_first(1, "block", xs, *rims, gain1, S, R)
+    fill_first(4, 4, "block", xs, *rims, gain1, S, R)
     halo.send_along()
-    halo.relay()
-    halo.receive_across(1)
+    halo.relay(1)
+    halo.relay(2)
+    halo.receive_across(0)
     loads[3].wait()
-    fill_first(1, "rims", xs, *rims, gain1, S, R)
-    build_first(1, S, B1, E1)
+    fill_first(4, 4, "rims", xs, *rims, gain1, S, R)
+    build_first(4, 4, S, B1, E1)
     for o in (4, 5):
         put_second(o, conv_first(o, 0, 3, B1, E1, W1), gain2, keep, Ta, Tb)
-    fill_first(0, "block", zb, *rims, gain1, S, R)
+    fill_first(0, 4, "block", zb, *rims, gain1, S, R)
     acc1[0] = conv_first(2, 2, 3, B1, E1, W1)
     acc1[1] = conv_first(3, 1, 3, B1, E1, W1)
     for o in (4, 5):
         build_second(o, Ta, Tb, *ops)
     for c in loads2:
         c.wait()
-    acc2[0] = conv_second(2, 27, 42, all_ops, W2)
-    acc2[1] = conv_second(3, 14, 42, all_ops, W2)
-    loads[4].wait()
-    halo.receive_relayed()
-
-    fill_first(0, "rims", zb, *rims, gain1, S, R)
-    build_first(0, S, B1, E1)
-    for o in (3, 2, 1, 0):
-        if o == 3:
-            hidden = acc1[1] + conv_first(3, 0, 1, B1, E1, W1)
-        elif o == 2:
-            hidden = acc1[0] + conv_first(2, 0, 2, B1, E1, W1)
-        else:
-            hidden = conv_first(o, 0, 3, B1, E1, W1)
-        put_second(o, hidden, gain2, keep, Ta, Tb)
+    halo.receive_relayed(1)
+
+    fill_first(2, 2, "rims", zb, *rims, gain1, S, R)
+    build_first(2, 2, S, B1, E1)
+    acc2[3] = conv_second(3, 14, 42, all_ops, W2)
+    acc2[2] = conv_second(2, 27, 42, all_ops, W2)
+    for o in (3, 2):
+        put_second(o, acc1[o - 2] + conv_first(o, 0, 4 - o, B1, E1, W1), gain2, keep, Ta, Tb)
         build_second(o, Ta, Tb, *ops)
         build_pair(o, Tb, P2f, P2fe)
-        if o == 3:
-            merged = acc2[1] + conv_second(3, 0, 14, all_ops, W2)
-        elif o == 2:
-            merged = acc2[0] + conv_second(2, 0, 27, all_ops, W2)
-        else:
-            merged = conv_second(o, 0, 42, all_ops, W2)
-        put_merged(o, merged, keep, Mg)
-    downscale(Mg, W3, Q, out)
+    loads[4].wait()
+    halo.receive_relayed(2)
+
+    fill_first(0, 2, "rims", zb, *rims, gain1, S, R)
+    build_first(0, 2, S, B1, E1)
+    put_merged(3, acc2[3] + conv_second(3, 0, 14, all_ops, W2), keep, Mg)
+    put_merged(2, acc2[2] + conv_second(2, 0, 27, all_ops, W2), keep, Mg)
+    put_second(1, conv_first(1, 0, 3, B1, E1, W1), gain2, keep, Ta, Tb)
+    acc2[1] = conv_second(1, 14, 42, all_ops, W2)
+    build_second(1, Ta, Tb, *ops)
+    build_pair(1, Tb, P2f, P2fe)
+    put_second(0, conv_first(0, 0, 3, B1, E1, W1), gain2, keep, Ta, Tb)
+    acc2[0] = conv_second(0, 14, 42, all_ops, W2)
+    downscale(2, 2, Mg, W3, Q, out)
+    put_merged(1, acc2[1] + conv_second(1, 0, 14, all_ops, W2), keep, Mg)
+    build_second(0, Ta, Tb, *ops)
+    build_pair(0, Tb, P2f, P2fe)
+    put_merged(0, acc2[0] + conv_second(0, 0, 14, all_ops, W2), keep, Mg)
+    downscale(0, 2, Mg, W3, Q, out)
     halo.finish()
 
 
@@ -461,18 +472,18 @@
         ((3, 3, 6, 16, 128), bf), ((3, 6, 16, 128), bf), ((6, 16, 128), bf), ((6, 16, 128), bf),
         ((4, 9, 16, 128), bf), ((4, 16, 128), bf),
         ((27, 128, 192), bf), ((42, 128, 192), bf), ((9, 256, 192), bf),
-        ((2, 4 * 9 * 32, 128), f32), ((2, 128, 128), f32), ((2, 224, 192), f32), ((2, 160, 192), f32),
+        ((2, 44 * 32, 128), f32), ((2, 192, 128), f32), ((2, 224, 192), f32), ((4, 160, 192), f32),
     ]
     return pl.pallas_call(
         field_kernel,
-        out_shape=[jax.ShapeDtypeStruct((4, 4, 1536), bf)] + [jax.ShapeDtypeStruct(s, bf) for s in LANDING],
+        out_shape=jax.ShapeDtypeStruct((4, 4, 1536), bf),
         in_specs=[HBM] * 7,
-        out_specs=[VM] * 7,
-        scratch_shapes=[pltpu.VMEM(*s) for s in shapes]
-        + [dma((5,)), dma((31,)), dma, dma, dma((2, 8)), dma((2, 8)), pltpu.SemaphoreType.REGULAR],
+        out_specs=VM,
+        scratch_shapes=[pltpu.VMEM(s, bf) for s in LANDING] + [pltpu.VMEM(*s) for s in shapes]
+        + [dma((5,)), dma((31,)), dma((3,)), dma((3,)), dma((3, 8)), dma((3, 8)), pltpu.SemaphoreType.REGULAR],
         compiler_params=pltpu.CompilerParams(
             collective_id=0, has_side_effects=True, vmem_limit_bytes=40 * 2**20),
-    )(x, g1, g2, k1, k2, sc, k3)[0]
+    )(x, g1, g2, k1, k2, sc, k3)
 
 
 def local(x, g1, g2, k1, k2, sc, dw):

time: 22 us -> 21 us (0.955)
  Pallas kernels: 21.2 us -> 20.3 us
    pallas_call x1, Pallas kernels: 21.2 us -> 20.3 us  [field(): pl.pallas_call(field_kernel, out_shape=jax.ShapeDtypeStruct((4, 4, 1536),...]
where the time goes in v4:
time: 21 us; the launch traced here: 20.9 us
  Pallas kernels  20.3 us (97%)
  local copies, waits for them, and re-layouts  0.62 us (3%)
    pallas_call x1, Pallas kernels, field(): pl.pallas_call(field_kernel, out_shape=jax.ShapeDtypeStruct((4, 4, 1536),...  20.3 us
    unnamed x1, local copies, waits for them, and re-layouts  0.62 us

profile of v4, /device:TPU:1, one launch (start us, length us, event | category | flops | bytes accessed | tf_op | source)
XLA Modules:
  0.0 20.9 jit_solution(10579193559617935454)
XLA Ops:
  0.0 20.3 %shard_map.73 = bf16[4,4,1536]{2,1,0:T(4,128)(2,1)S(1)} custom-call(bf16[4,8,1536]{2,1,0:T(8,128)(2,1)} %x.1, f32[1,96]{1,0:T(1,128)} %bitcast.9, f32[1,192]{1,0:T(1,128)} %bitcast.8, bf16[27,96,192]{2,1,0:T(8,128)(2,1)} %bitcast.6, bf16[27,192,192]{2,1,0:T(8,128)(2,1)} %bitcast.5, bf16[96,192]{1,0:T(8,128)(2,1)} %sc.1, bf16[9,192,192]{2,1,0:T(8,128)(2,1)} %bitcast.7), custom_call_target="tpu_custom_call" | custom-call | tf_op jit(solution)/shard_map/pallas_call | solution.py:477
  20.3 0.6 %copy.9 = bf16[4,4,1536]{2,1,0:T(4,128)(2,1)} copy(bf16[4,4,1536]{2,1,0:T(4,128)(2,1)S(1)} %shard_map.73) | data formatting | bytes 98304
